TPU v7x, 32 devices: a whole 2x2x4 slice. The times are simulated.
32 devices in a mesh: dp: 2 (over y), fsdp: 16 (over z, x, core).
Axes of the slice: x: 2, y: 2, z: 4, core: 2. Of those that a mesh axis runs over, the one named last changes fastest.
Arguments:
- patches: bfloat16 [160, 197, 768], P(('dp', 'fsdp')), may hold values from -6 to 6
- patch_mask: int32 [160, 197], P(('dp', 'fsdp')), may hold values from 0 to 1, as said below
- cotangent: bfloat16 [160, 197, 768], P(('dp', 'fsdp')), may hold values from -6 to 6
- mask_token: bfloat16 [768], P(('dp', 'fsdp')), may hold values from -5 to 5
- pre_gain: bfloat16 [768], P(('dp', 'fsdp')), may hold values from 0.099609375 to 1.8984375
- pre_shift: bfloat16 [768], P(('dp', 'fsdp')), may hold values from -3 to 3
- qkv_weight: bfloat16 [1769472], P(('dp', 'fsdp')), may hold values from -0.21875 to 0.21875
- query_bias: bfloat16 [768], P(('dp', 'fsdp')), may hold values from -3 to 3
- value_bias: bfloat16 [768], P(('dp', 'fsdp')), may hold values from -3 to 3
- rel_table: bfloat16 [8800], P(('dp', 'fsdp')), may hold values from -4 to 4
- out_weight: bfloat16 [589824], P(('dp', 'fsdp')), may hold values from -1.25 to 1.25
- out_bias: bfloat16 [768], P(('dp', 'fsdp')), may hold values from -3 to 3
- attn_scale: bfloat16 [768], P(('dp', 'fsdp')), may hold values from 0.099609375 to 1.8984375
- post_gain: bfloat16 [768], P(('dp', 'fsdp')), may hold values from 0.099609375 to 1.8984375
- post_shift: bfloat16 [768], P(('dp', 'fsdp')), may hold values from -3 to 3
- up_weight: bfloat16 [2359296], P(('dp', 'fsdp')), may hold values from -0.21875 to 0.21875
- up_bias: bfloat16 [3072], P(('dp', 'fsdp')), may hold values from -3 to 3
- down_weight: bfloat16 [2359296], P(('dp', 'fsdp')), may hold values from -0.109375 to 0.109375
- down_bias: bfloat16 [768], P(('dp', 'fsdp')), may hold values from -3 to 3
- mlp_scale: bfloat16 [768], P(('dp', 'fsdp')), may hold values from 0.099609375 to 1.8984375
Outputs:
- layer_out: bfloat16 [160, 197, 768], P(('dp', 'fsdp'))
- patch_grad: bfloat16 [160, 197, 768], P(('dp', 'fsdp'))
- mask_token_grad: float32 [768], P(('dp', 'fsdp'))
- pre_gain_grad: float32 [768], P(('dp', 'fsdp'))
- pre_shift_grad: float32 [768], P(('dp', 'fsdp'))
- qkv_weight_grad: float32 [1769472], P(('dp', 'fsdp'))
- query_bias_grad: float32 [768], P(('dp', 'fsdp'))
- value_bias_grad: float32 [768], P(('dp', 'fsdp'))
- rel_table_grad: float32 [8800], P(('dp', 'fsdp'))
- out_weight_grad: float32 [589824], P(('dp', 'fsdp'))
- out_bias_grad: float32 [768], P(('dp', 'fsdp'))
- attn_scale_grad: float32 [768], P(('dp', 'fsdp'))
- post_gain_grad: float32 [768], P(('dp', 'fsdp'))
- post_shift_grad: float32 [768], P(('dp', 'fsdp'))
- up_weight_grad: float32 [2359296], P(('dp', 'fsdp'))
- up_bias_grad: float32 [3072], P(('dp', 'fsdp'))
- down_weight_grad: float32 [2359296], P(('dp', 'fsdp'))
- down_bias_grad: float32 [768], P(('dp', 'fsdp'))
- mlp_scale_grad: float32 [768], P(('dp', 'fsdp'))
Inputs may be any that keep to these rules, and one draw needn't show every extreme that they name: `patch_mask`: row 0 (the class token) of every image is 0 and every image has at least one masked patch.
All inputs are finite; a program needn't handle non-finite values.
Results may differ from a plain program's by a relative error of at most 0.012.
Values may be sent and summed in bfloat16 or wider, within the bound.
A program may use at most 192 MiB of HBM per device.

v0:
```python
import math

import jax
import jax.numpy as jnp
from jax import lax
from jax.sharding import PartitionSpec as P

HEADS = 12
FF = 3072
GRID = 14


norm_eps = 1e-06
block_rows = 16


def relative_index(row_ids, col_ids, grid_side):
    table_rows = (2 * grid_side - 1) ** 2 + 3
    rel_rows = row_ids - 1
    rel_cols = col_ids - 1
    down_diff = rel_rows // grid_side - rel_cols // grid_side + grid_side - 1
    across_diff = rel_rows % grid_side - rel_cols % grid_side + grid_side - 1
    inside = down_diff * (2 * grid_side - 1) + across_diff
    first_row = row_ids == 0
    first_col = col_ids == 0
    position = jnp.where(first_row, table_rows - 3, jnp.where(first_col, table_rows - 2, inside))
    position = jnp.where(first_row & first_col, table_rows - 1, position)
    return position


def position_onehot(block_id, seq_len, grid_side, table_rows):
    row_ids = block_id * block_rows + jnp.arange(block_rows, dtype=jnp.int32)
    col_ids = jnp.arange(seq_len, dtype=jnp.int32)
    position = relative_index(row_ids[:, None], col_ids[None, :], grid_side)
    position = jnp.where(row_ids[:, None] < seq_len, position, -1)
    table_ids = jnp.arange(table_rows, dtype=jnp.int32)
    onehot = (position[:, :, None] == table_ids[None, None, :]).astype(jnp.bfloat16)
    return onehot.reshape(block_rows * seq_len, table_rows)


def unpack(flat, shape):
    entries = math.prod(shape)
    return flat[:entries].reshape(shape)


def pad_flat(values, length):
    flat = values.reshape(-1)
    return jnp.pad(flat, (0, length - flat.shape[0]))


def normalize(values):
    average = jnp.mean(values, axis=-1, keepdims=True)
    centred = values - average
    variance = jnp.mean(centred * centred, axis=-1, keepdims=True)
    inverse = lax.rsqrt(variance + norm_eps)
    return (centred * inverse, inverse)


def norm_back(grad_normed, normal, inverse, gain):
    scaled = grad_normed * gain
    first_mean = jnp.mean(scaled, axis=-1, keepdims=True)
    second_mean = jnp.mean(scaled * normal, axis=-1, keepdims=True)
    return inverse * (scaled - first_mean - normal * second_mean)


def gelu_slope(values):
    return (
        0.5 * (1.0 + lax.erf(values * 0.7071067811865476))
        + values * jnp.exp(-0.5 * values * values) * 0.3989422804014327
    )


def attn_unpack(full, model_dim, table_rows, heads):
    wide = [piece.astype(jnp.float32) for piece in full]
    return (
        wide[0],
        wide[1],
        wide[2],
        unpack(full[3], (model_dim, 3 * model_dim)),
        wide[4],
        wide[5],
        unpack(full[6], (table_rows, heads)),
        unpack(full[7], (model_dim, model_dim)),
        wide[8],
        wide[9],
    )


def mlp_unpack(full, model_dim, hidden_dim):
    wide = [piece.astype(jnp.float32) for piece in full]
    return (
        wide[0],
        wide[1],
        unpack(full[2], (model_dim, hidden_dim)),
        wide[3],
        unpack(full[4], (hidden_dim, model_dim)),
        wide[5],
        wide[6],
    )


def per_device(
    patches,
    patch_mask,
    cotangent,
    mask_token,
    pre_gain,
    pre_shift,
    qkv_weight,
    query_bias,
    value_bias,
    rel_table,
    out_weight,
    out_bias,
    attn_scale,
    post_gain,
    post_shift,
    up_weight,
    up_bias,
    down_weight,
    down_bias,
    mlp_scale,
):
    images, seq_len, model_dim = patches.shape
    heads = HEADS
    head_dim = model_dim // heads
    hidden_dim = FF
    grid_side = GRID
    table_rows = (2 * GRID - 1) ** 2 + 3
    block_count = -(-seq_len // block_rows)
    padded_rows = block_count * block_rows
    four_dims = (images, seq_len, heads, head_dim)
    total_devices = lax.axis_size(("dp", "fsdp"))
    attn_shards = (
        mask_token,
        pre_gain,
        pre_shift,
        qkv_weight,
        query_bias,
        value_bias,
        rel_table,
        out_weight,
        out_bias,
        attn_scale,
    )
    mlp_shards = (post_gain, post_shift, up_weight, up_bias, down_weight, down_bias, mlp_scale)
    attn_full = (
        lax.all_gather(mask_token, ("dp", "fsdp"), axis=0, tiled=True),
        lax.all_gather(pre_gain, ("dp", "fsdp"), axis=0, tiled=True),
        lax.all_gather(pre_shift, ("dp", "fsdp"), axis=0, tiled=True),
        lax.all_gather(qkv_weight, ("dp", "fsdp"), axis=0, tiled=True),
        lax.all_gather(query_bias, ("dp", "fsdp"), axis=0, tiled=True),
        lax.all_gather(value_bias, ("dp", "fsdp"), axis=0, tiled=True),
        lax.all_gather(rel_table, ("dp", "fsdp"), axis=0, tiled=True),
        lax.all_gather(out_weight, ("dp", "fsdp"), axis=0, tiled=True),
        lax.all_gather(out_bias, ("dp", "fsdp"), axis=0, tiled=True),
        lax.all_gather(attn_scale, ("dp", "fsdp"), axis=0, tiled=True),
    )
    token_fill, pre_g, pre_s, qkv_w, query_b, value_b, table, out_w, out_b, attn_g = attn_unpack(
        attn_full, model_dim, table_rows, heads
    )
    masked = patch_mask.reshape(-1, 1) == 1
    token_rows = patches.reshape(-1, model_dim).astype(jnp.float32)
    initial = jnp.where(masked, token_fill[None, :], token_rows)
    normal_pre, inverse_pre = normalize(initial)
    normed_pre = (normal_pre * pre_g + pre_s).astype(jnp.bfloat16)
    projected = jnp.dot(normed_pre, qkv_w, preferred_element_type=jnp.float32)
    queries = ((projected[:, :model_dim] + query_b) * 0.125).astype(jnp.bfloat16).reshape(four_dims)
    keys_all = projected[:, model_dim : 2 * model_dim].astype(jnp.bfloat16).reshape(four_dims)
    values_all = (projected[:, 2 * model_dim :] + value_b).astype(jnp.bfloat16).reshape(four_dims)

    def bias_rows(block_id):
        onehot = position_onehot(block_id, seq_len, grid_side, table_rows)
        return jnp.einsum("rh,ar->ha", table, onehot, preferred_element_type=jnp.float32)

    bias_pieces = lax.map(bias_rows, jnp.arange(block_count, dtype=jnp.int32))
    bias_pieces = bias_pieces.reshape(block_count, heads, block_rows, seq_len)
    pos_bias = jnp.transpose(bias_pieces, (1, 0, 2, 3)).reshape(heads, padded_rows, seq_len)[
        :, :seq_len
    ]
    scores = (
        jnp.einsum("ishd,ithd->ihst", queries, keys_all, preferred_element_type=jnp.float32)
        + pos_bias[None]
    )
    peak = jnp.max(scores, axis=-1, keepdims=True)
    shifted = jnp.exp(scores - peak)
    totals = jnp.sum(shifted, axis=-1, keepdims=True)
    probs = shifted / totals
    log_total = peak + jnp.log(totals)
    attended = jnp.einsum(
        "ihst,ithd->ishd",
        probs.astype(jnp.bfloat16),
        values_all,
        preferred_element_type=jnp.float32,
    )
    attended = attended.reshape(-1, model_dim).astype(jnp.bfloat16)
    branch = jnp.dot(attended, out_w, preferred_element_type=jnp.float32) + out_b
    middle = initial + attn_g * branch
    mlp_full = (
        lax.all_gather(post_gain, ("dp", "fsdp"), axis=0, tiled=True),
        lax.all_gather(post_shift, ("dp", "fsdp"), axis=0, tiled=True),
        lax.all_gather(up_weight, ("dp", "fsdp"), axis=0, tiled=True),
        lax.all_gather(up_bias, ("dp", "fsdp"), axis=0, tiled=True),
        lax.all_gather(down_weight, ("dp", "fsdp"), axis=0, tiled=True),
        lax.all_gather(down_bias, ("dp", "fsdp"), axis=0, tiled=True),
        lax.all_gather(mlp_scale, ("dp", "fsdp"), axis=0, tiled=True),
    )
    post_g, post_s, up_w, up_b, down_w, down_b, mlp_g = mlp_unpack(mlp_full, model_dim, hidden_dim)
    normal_post, inverse_post = normalize(middle)
    normed_post = (normal_post * post_g + post_s).astype(jnp.bfloat16)
    up_rows = jnp.dot(normed_post, up_w, preferred_element_type=jnp.float32) + up_b
    hidden = jax.nn.gelu(up_rows, approximate=False).astype(jnp.bfloat16)
    down_rows = jnp.dot(hidden, down_w, preferred_element_type=jnp.float32) + down_b
    result = middle + mlp_g * down_rows
    layer_out = result.astype(jnp.bfloat16).reshape(patches.shape)
    mlp_second = (
        lax.all_gather(post_gain, ("dp", "fsdp"), axis=0, tiled=True),
        lax.all_gather(post_shift, ("dp", "fsdp"), axis=0, tiled=True),
        lax.all_gather(up_weight, ("dp", "fsdp"), axis=0, tiled=True),
        lax.all_gather(up_bias, ("dp", "fsdp"), axis=0, tiled=True),
        lax.all_gather(down_weight, ("dp", "fsdp"), axis=0, tiled=True),
        lax.all_gather(down_bias, ("dp", "fsdp"), axis=0, tiled=True),
        lax.all_gather(mlp_scale, ("dp", "fsdp"), axis=0, tiled=True),
    )
    post_g, post_s, up_w, up_b, down_w, down_b, mlp_g = mlp_unpack(
        mlp_second, model_dim, hidden_dim
    )
    grad_out = cotangent.reshape(-1, model_dim).astype(jnp.float32) * masked.astype(jnp.float32)
    mlp_scale_grad = jnp.sum(grad_out * down_rows, axis=0)
    grad_down_rows = mlp_g * grad_out
    down_bias_grad = jnp.sum(grad_down_rows, axis=0)
    grad_down = grad_down_rows.astype(jnp.bfloat16)
    down_weight_grad = jnp.einsum(
        "ra,rb->ab", hidden, grad_down, preferred_element_type=jnp.float32
    )
    grad_hidden = jnp.einsum("rb,ab->ra", grad_down, down_w, preferred_element_type=jnp.float32)
    grad_up_rows = grad_hidden * gelu_slope(up_rows)
    up_bias_grad = jnp.sum(grad_up_rows, axis=0)
    grad_up = grad_up_rows.astype(jnp.bfloat16)
    up_weight_grad = jnp.einsum(
        "ra,rb->ab", normed_post, grad_up, preferred_element_type=jnp.float32
    )
    grad_normed_post = jnp.einsum("rb,ab->ra", grad_up, up_w, preferred_element_type=jnp.float32)
    post_gain_grad = jnp.sum(grad_normed_post * normal_post, axis=0)
    post_shift_grad = jnp.sum(grad_normed_post, axis=0)
    grad_middle = grad_out + norm_back(grad_normed_post, normal_post, inverse_post, post_g)
    mlp_lists = (
        post_gain_grad,
        post_shift_grad,
        up_weight_grad,
        up_bias_grad,
        down_weight_grad,
        down_bias_grad,
        mlp_scale_grad,
    )
    mlp_flat = [
        pad_flat(grad, shard.shape[0] * total_devices) for grad, shard in zip(mlp_lists, mlp_shards)
    ]
    mlp_owned = (
        lax.psum_scatter(mlp_flat[0], ("dp", "fsdp"), scatter_dimension=0, tiled=True),
        lax.psum_scatter(mlp_flat[1], ("dp", "fsdp"), scatter_dimension=0, tiled=True),
        lax.psum_scatter(mlp_flat[2], ("dp", "fsdp"), scatter_dimension=0, tiled=True),
        lax.psum_scatter(mlp_flat[3], ("dp", "fsdp"), scatter_dimension=0, tiled=True),
        lax.psum_scatter(mlp_flat[4], ("dp", "fsdp"), scatter_dimension=0, tiled=True),
        lax.psum_scatter(mlp_flat[5], ("dp", "fsdp"), scatter_dimension=0, tiled=True),
        lax.psum_scatter(mlp_flat[6], ("dp", "fsdp"), scatter_dimension=0, tiled=True),
    )
    attn_second = (
        lax.all_gather(mask_token, ("dp", "fsdp"), axis=0, tiled=True),
        lax.all_gather(pre_gain, ("dp", "fsdp"), axis=0, tiled=True),
        lax.all_gather(pre_shift, ("dp", "fsdp"), axis=0, tiled=True),
        lax.all_gather(qkv_weight, ("dp", "fsdp"), axis=0, tiled=True),
        lax.all_gather(query_bias, ("dp", "fsdp"), axis=0, tiled=True),
        lax.all_gather(value_bias, ("dp", "fsdp"), axis=0, tiled=True),
        lax.all_gather(rel_table, ("dp", "fsdp"), axis=0, tiled=True),
        lax.all_gather(out_weight, ("dp", "fsdp"), axis=0, tiled=True),
        lax.all_gather(out_bias, ("dp", "fsdp"), axis=0, tiled=True),
        lax.all_gather(attn_scale, ("dp", "fsdp"), axis=0, tiled=True),
    )
    token_fill, pre_g, pre_s, qkv_w, query_b, value_b, table, out_w, out_b, attn_g = attn_unpack(
        attn_second, model_dim, table_rows, heads
    )
    attn_scale_grad = jnp.sum(grad_middle * branch, axis=0)
    grad_branch_rows = attn_g * grad_middle
    out_bias_grad = jnp.sum(grad_branch_rows, axis=0)
    grad_branch = grad_branch_rows.astype(jnp.bfloat16)
    out_weight_grad = jnp.einsum(
        "ra,rb->ab", attended, grad_branch, preferred_element_type=jnp.float32
    )
    grad_attended = jnp.einsum("rb,ab->ra", grad_branch, out_w, preferred_element_type=jnp.float32)
    grad_attended = grad_attended.astype(jnp.bfloat16).reshape(four_dims)
    scores_again = (
        jnp.einsum("ishd,ithd->ihst", queries, keys_all, preferred_element_type=jnp.float32)
        + pos_bias[None]
    )
    probs_again = jnp.exp(scores_again - log_total)
    grad_probs = jnp.einsum(
        "ishd,ithd->ihst", grad_attended, values_all, preferred_element_type=jnp.float32
    )
    grad_values = jnp.einsum(
        "ihst,ishd->ithd",
        probs_again.astype(jnp.bfloat16),
        grad_attended,
        preferred_element_type=jnp.float32,
    )
    inner_sum = jnp.sum(probs_again * grad_probs, axis=-1, keepdims=True)
    grad_scores = probs_again * (grad_probs - inner_sum)
    bias_grad = jnp.sum(grad_scores, axis=0)
    grad_scores_low = grad_scores.astype(jnp.bfloat16)
    grad_queries = (
        jnp.einsum("ihst,ithd->ishd", grad_scores_low, keys_all, preferred_element_type=jnp.float32)
        * 0.125
    )
    grad_keys = jnp.einsum(
        "ihst,ishd->ithd", grad_scores_low, queries, preferred_element_type=jnp.float32
    )
    grad_queries = grad_queries.reshape(-1, model_dim)
    grad_keys = grad_keys.reshape(-1, model_dim)
    grad_values = grad_values.reshape(-1, model_dim)
    query_bias_grad = jnp.sum(grad_queries, axis=0)
    value_bias_grad = jnp.sum(grad_values, axis=0)
    grad_projected = jnp.concatenate([grad_queries, grad_keys, grad_values], axis=1).astype(
        jnp.bfloat16
    )
    qkv_weight_grad = jnp.einsum(
        "ra,rb->ab", normed_pre, grad_projected, preferred_element_type=jnp.float32
    )
    grad_normed_pre = jnp.einsum(
        "rb,ab->ra", grad_projected, qkv_w, preferred_element_type=jnp.float32
    )
    pre_gain_grad = jnp.sum(grad_normed_pre * normal_pre, axis=0)
    pre_shift_grad = jnp.sum(grad_normed_pre, axis=0)
    grad_initial = grad_middle + norm_back(grad_normed_pre, normal_pre, inverse_pre, pre_g)
    mask_token_grad = jnp.sum(jnp.where(masked, grad_initial, 0.0), axis=0)
    patch_grad = jnp.where(masked, 0.0, grad_initial).astype(jnp.bfloat16).reshape(patches.shape)
    bias_grid = jnp.pad(bias_grad, ((0, 0), (0, padded_rows - seq_len), (0, 0)))
    bias_grid = bias_grid.reshape(heads, block_count, block_rows * seq_len)
    bias_grid = jnp.transpose(bias_grid, (1, 0, 2))

    def add_block(running, inputs):
        block_id, piece = inputs
        onehot = position_onehot(block_id, seq_len, grid_side, table_rows)
        upper = piece.astype(jnp.bfloat16)
        lower = (piece - upper.astype(jnp.float32)).astype(jnp.bfloat16)
        running = running + jnp.dot(upper, onehot, preferred_element_type=jnp.float32)
        running = running + jnp.dot(lower, onehot, preferred_element_type=jnp.float32)
        return (running, None)

    table_grad_t, _ = lax.scan(
        add_block,
        jnp.zeros((heads, table_rows), jnp.float32),
        (jnp.arange(block_count, dtype=jnp.int32), bias_grid),
    )
    table_grad = jnp.transpose(table_grad_t)
    attn_lists = (
        mask_token_grad,
        pre_gain_grad,
        pre_shift_grad,
        qkv_weight_grad,
        query_bias_grad,
        value_bias_grad,
        table_grad,
        out_weight_grad,
        out_bias_grad,
        attn_scale_grad,
    )
    attn_flat = [
        pad_flat(grad, shard.shape[0] * total_devices)
        for grad, shard in zip(attn_lists, attn_shards)
    ]
    attn_owned = (
        lax.psum_scatter(attn_flat[0], ("dp", "fsdp"), scatter_dimension=0, tiled=True),
        lax.psum_scatter(attn_flat[1], ("dp", "fsdp"), scatter_dimension=0, tiled=True),
        lax.psum_scatter(attn_flat[2], ("dp", "fsdp"), scatter_dimension=0, tiled=True),
        lax.psum_scatter(attn_flat[3], ("dp", "fsdp"), scatter_dimension=0, tiled=True),
        lax.psum_scatter(attn_flat[4], ("dp", "fsdp"), scatter_dimension=0, tiled=True),
        lax.psum_scatter(attn_flat[5], ("dp", "fsdp"), scatter_dimension=0, tiled=True),
        lax.psum_scatter(attn_flat[6], ("dp", "fsdp"), scatter_dimension=0, tiled=True),
        lax.psum_scatter(attn_flat[7], ("dp", "fsdp"), scatter_dimension=0, tiled=True),
        lax.psum_scatter(attn_flat[8], ("dp", "fsdp"), scatter_dimension=0, tiled=True),
        lax.psum_scatter(attn_flat[9], ("dp", "fsdp"), scatter_dimension=0, tiled=True),
    )
    return (
        layer_out,
        patch_grad,
        attn_owned[0],
        attn_owned[1],
        attn_owned[2],
        attn_owned[3],
        attn_owned[4],
        attn_owned[5],
        attn_owned[6],
        attn_owned[7],
        attn_owned[8],
        attn_owned[9],
        mlp_owned[0],
        mlp_owned[1],
        mlp_owned[2],
        mlp_owned[3],
        mlp_owned[4],
        mlp_owned[5],
        mlp_owned[6],
    )


def solution(mesh):
    in_specs = (
        P(("dp", "fsdp"), None, None),
        P(("dp", "fsdp"), None),
        P(("dp", "fsdp"), None, None),
        P(("dp", "fsdp")),
        P(("dp", "fsdp")),
        P(("dp", "fsdp")),
        P(("dp", "fsdp")),
        P(("dp", "fsdp")),
        P(("dp", "fsdp")),
        P(("dp", "fsdp")),
        P(("dp", "fsdp")),
        P(("dp", "fsdp")),
        P(("dp", "fsdp")),
        P(("dp", "fsdp")),
        P(("dp", "fsdp")),
        P(("dp", "fsdp")),
        P(("dp", "fsdp")),
        P(("dp", "fsdp")),
        P(("dp", "fsdp")),
        P(("dp", "fsdp")),
    )
    out_specs = (
        P(("dp", "fsdp"), None, None),
        P(("dp", "fsdp"), None, None),
        P(("dp", "fsdp")),
        P(("dp", "fsdp")),
        P(("dp", "fsdp")),
        P(("dp", "fsdp")),
        P(("dp", "fsdp")),
        P(("dp", "fsdp")),
        P(("dp", "fsdp")),
        P(("dp", "fsdp")),
        P(("dp", "fsdp")),
        P(("dp", "fsdp")),
        P(("dp", "fsdp")),
        P(("dp", "fsdp")),
        P(("dp", "fsdp")),
        P(("dp", "fsdp")),
        P(("dp", "fsdp")),
        P(("dp", "fsdp")),
        P(("dp", "fsdp")),
    )
    return jax.shard_map(
        per_device, mesh=mesh, in_specs=in_specs, out_specs=out_specs, check_vma=False
    )
```

profile of v0, /device:TPU:0, one launch (start us, length us, event | category | flops | bytes accessed | tf_op | source)
XLA Modules:
  0.0 1161.2 jit_solution(9162443884220730028)
XLA Ops:
  16.7 43.0 %all-reduce.34 = (bf16[768]{0:T(1024)(128)(2,1)S(1)}, bf16[768]{0:T(1024)(128)(2,1)S(1)}, bf16[768]{0:T(1024)(128)(2,1)S(1)}, bf16[768]{0:T(1024)(128)(2,1)S(1)}...) all-reduce(bf16[768]{0:T(1024)(128)(2,1)S(1)} %dynamic-update-slice, ...), channel_id=1, replica_groups=mesh['dp'=2,'fsdp'=16] {'dp','fsdp'}, use_global_device_ids=true, to_apply=%add.5 | all-reduce | flops 20320 | bytes 81280
  65.7 66.2 %while.31 = (s32[]{:T(128)}, f32[13,12,3152]{2,1,0:T(8,128)}, s32[13]{0:T(128)S(1)}, bf16[732,12]{0,1:T(8,128)(2,1)S(1)}, s32[]{:T(128)}, /*index=5*/s32[1]{0:T(128)}) while((s32[]{:T(128)}, f32[13,12,3152]{2,1,0:T(8,128)}, s32[13]{0:T(128)S(1)}, bf16[732,12]{0,1:T(8,128)(2,1)S(1)}, s32[]{:T(128)}, /*index=5*/s32[1]{0:T(128)}) %tuple.122), condition=%wide.region_3.4_spmd, body=%wide.region_2.3_spmd.sunk | while | flops 57719896 | bytes 491115 | solution.py:176
  156.4 8.0 reshape.798
  210.2 8.5 add_reduce_fusion
  218.6 7.7 fusion.43
  226.4 7.4 convert_bitcast_fusion.1
  251.0 8.2 reshape.806
  259.3 35.7 %fusion.30 = (bf16[985,3072]{1,0:T(8,128)(2,1)}, f32[985,3072]{1,0:T(8,128)}) fusion(f32[3072]{0:T(1024)S(1)} %convert_element_type.195, bf16[768,3072]{1,0:T(8,128)(2,1)} %reshape.806, f32[985,768]{1,0:T(8,128)} %copy-done.1, f32[768]{0:T(1024)S(1)} %convert_element_type.193, f32[768]{0:T(1024)S(1)} %convert_element_type.192, ...), kind=kOutput, calls=%fused_computation.58 | convolution fusion | flops 4851306496 | bytes 25926344 | tf_op jit(solution)/shard_map/dot_general | solution.py:211
  295.0 9.3 reshape.807
  304.3 12.9 %fusion.75 = (f32[3072]{0:T(1024)}, bf16[985,3072]{1,0:T(8,128)(2,1)S(1)}) fusion(f32[985,3072]{1,0:T(8,128)} %get-tuple-element.366, f32[3072]{0:T(1024)S(1)} %convert_element_type.195, bf16[985,768]{1,0:T(8,128)(2,1)} %convert_element_type.205, bf16[3072,768]{1,0:T(8,128)(2,1)} %reshape.807), kind=kOutput, calls=%fused_computation.159 | convolution fusion | flops 4684121088 | bytes 24411648 | tf_op jit(solution)/shard_map/rb,ab->ra/dot_general | solution.py:236
  317.2 12.2 %multiply_reduce_fusion.3 = (f32[768]{0:T(1024)}, f32[985]{0:T(1024)S(1)}, f32[985]{0:T(1024)S(1)}, f32[768]{0:T(1024)}, f32[985,768]{1,0:T(8,128)}) fusion(f32[985,768]{1,0:T(8,128)S(1)} %copy-done.2, f32[985]{0:T(1024)S(1)} %add_rsqrt_fusion.1, f32[985]{0:T(1024)S(1)} %broadcast_multiply_fusion.5, f32[768]{0:T(1024)S(1)} %convert_element_type.192, ...), kind=kOutput, calls=%fused_computation.106 | convolution fusion | flops 4654619648 | bytes 16847248 | tf_op jit(solution)/shard_map/rb,ab->ra/dot_general | solution.py:243
  329.5 10.2 multiply_reduce_fusion.4
  356.1 13.2 %multiply_reduce_fusion = (f32[5,12,197]{2,1,0:T(8,128)S(1)}, f32[5,12,197,197]{2,3,1,0:T(8,128)}) fusion(f32[5,12,197,197]{2,3,1,0:T(8,128)} %get-tuple-element.362, f32[5,12,197]{2,1,0:T(8,128)S(1)} %log_add_fusion, f32[12,197,197]{1,2,0:T(8,128)S(1)} %copy.84, bf16[5,197,12,64]{1,3,2,0:T(8,128)(2,1)} %copy.89, bf16[5,197,12,64]{1,3,2,0:T(8,128)(2,1)} %copy.85), kind=kOutput, calls=%fused_computation.52 | convolution fusion | flops 307355456 | bytes 23611632 | tf_op jit(solution)/shard_map/ishd,ithd->ihst/dot_general | solution.py:297
  369.3 11.6 fusion.72
  422.4 10.6 multiply_reduce_fusion.5
  433.0 7.5 fusion.64
  440.6 8.8 convolution_bitcast_fusion
  449.4 8.1 fusion.65
  472.9 98.9 %while.32 = (s32[]{:T(128)}, f32[12,732]{1,0:T(8,128)S(1)}, f32[13,12,3152]{2,0,1:T(8,128)}, s32[13]{0:T(128)S(1)}, s32[]{:T(128)}, /*index=5*/s32[1]{0:T(128)}, s32[]{:T(128)}) while((s32[]{:T(128)}, f32[12,732]{1,0:T(8,128)S(1)}, f32[13,12,3152]{2,0,1:T(8,128)}, s32[13]{0:T(128)S(1)}, s32[]{:T(128)}, /*index=5*/s32[1]{0:T(128)}, ...), condition=%wide.region_26.27_spmd.clone, body=%wide.region_25.26_spmd.clone.sunk | while | flops 115579144 | bytes 1027101 | solution.py:349
  581.7 8.0 reshape.814
  591.2 9.6 copy.118
  600.8 10.8 reshape.819
  616.5 90.3 %all-reduce.38.cloned.1.call-done = (f32[768]{0:T(1024)}, f32[768]{0:T(1024)}, f32[768]{0:T(1024)}, f32[768]{0:T(1024)}, f32[768]{0:T(1024)}, /*index=5*/f32[880...) async-done(((f32[768]{0:T(1024)}, f32[768]{0:T(1024)}, f32[768]{0:T(1024)}, ...) | async-done | bytes 81296
  723.3 424.1 %all-reduce.40.cloned.1.call-done = (f32[1769472]{0:T(1024)}, f32[589824]{0:T(1024)}, f32[2359296]{0:T(1024)}, f32[2359296]{0:T(1024)}) async-done(((f32[1769472]{0:T(1024)}, f32[589824]{0:T(1024)}, f32[2359296]{0:T(1024)}, f32[2359296]{0:T(1024)}), (f32[1769472]{0:T(1024)}, f32[589824]{0:T(1024)}, f32[2359296]{0:T(1024)}, f32[2359296]{0:T(1024)})) %all-reduce.40.cloned.1.call-update) | async-done | bytes 28311568
  (862 shorter events, 360.8 us)
Async XLA Ops:
  7.2 52.7 %copy-start.5 = (bf16[5,197,768]{2,1,0:T(8,128)(2,1)S(1)}, bf16[5,197,768]{2,1,0:T(8,128)(2,1)}, u32[]{:S(2)}) copy-start(bf16[5,197,768]{2,1,0:T(8,128)(2,1)} %param.24) | copy-start | bytes 4538884
  7.3 52.4 %copy-start.34 = (s32[5,197]{1,0:T(8,128)S(1)}, s32[5,197]{1,0:T(8,128)}, u32[]{:S(2)}) copy-start(s32[5,197]{1,0:T(8,128)} %param.25) | copy-start | bytes 11824
  7.3 145.7 %all-gather.7.cloned.1.call-start = ((), (), s32[]{:S(2)}) async-start(), calls=%async_computation.1 | async-start | bytes 1216512 | tf_op jit(solution)/shard_map/all_gather | solution.py:155
  8.1 148.4 %all-gather.5.cloned.1.call-start = ((), (), s32[]{:S(2)}) async-start(), calls=%async_computation | async-start | bytes 3649536 | tf_op jit(solution)/shard_map/all_gather | solution.py:151
  8.8 242.2 %all-gather.9.cloned.1.call-start = ((), (), s32[]{:S(2)}) async-start(), calls=%async_computation.2 | async-start | bytes 4866048 | tf_op jit(solution)/shard_map/all_gather | solution.py:202
  9.6 285.5 %all-gather.11.cloned.1.call-start = ((), (), s32[]{:S(2)}) async-start(), calls=%async_computation.3 | async-start | bytes 4866048 | tf_op jit(solution)/shard_map/all_gather | solution.py:204
  10.1 696.6 %all-reduce.38.cloned.1.call-start = ((), (), s32[]{:S(2)}) async-start(), calls=%async_computation.4 | async-start | bytes 188416
  59.8 182.9 %copy-start.21 = (f32[768]{0:T(1024)}, f32[768]{0:T(1024)S(1)}, u32[]{:S(2)}) copy-start(f32[768]{0:T(1024)S(1)} %convert_element_type.173) | copy-start | bytes 9220
  59.9 182.8 %copy-start.26 = (pred[985]{0:T(1024)(128)(4,1)}, pred[985]{0:T(1024)(128)(4,1)S(1)}, u32[]{:S(2)}) copy-start(pred[985]{0:T(1024)(128)(4,1)S(1)} %eq.137) | copy-start | bytes 2959
  141.0 228.3 %copy-start = (f32[12,197,197]{1,2,0:T(8,128)}, f32[12,197,197]{1,2,0:T(8,128)S(1)}, u32[]{:S(2)}) copy-start(f32[12,197,197]{1,2,0:T(8,128)S(1)} %copy.84) | copy-start | bytes 5588500
  304.3 12.9 %copy-start.2 = (f32[985,768]{1,0:T(8,128)S(1)}, f32[985,768]{1,0:T(8,128)}, u32[]{:S(2)}) copy-start(f32[985,768]{1,0:T(8,128)} %copy-done.1) | copy-start | bytes 9077764
  317.2 12.2 %copy-start.9 = (bf16[985,3072]{1,0:T(8,128)(2,1)}, bf16[985,3072]{1,0:T(8,128)(2,1)S(1)}, u32[]{:S(2)}) copy-start(bf16[985,3072]{1,0:T(8,128)(2,1)S(1)} %get-tuple-element.375) | copy-start | bytes 18155524
  317.2 12.2 %copy-start.14 = (bf16[3072,768]{1,0:T(8,128)(2,1)S(1)}, bf16[3072,768]{1,0:T(8,128)(2,1)}, u32[]{:S(2)}) copy-start(bf16[3072,768]{1,0:T(8,128)(2,1)} %reshape.807) | copy-start | bytes 14155780
  317.2 12.2 %copy-start.16 = (f32[985,768]{1,0:T(8,128)S(1)}, f32[985,768]{1,0:T(8,128)}, u32[]{:S(2)}) copy-start(f32[985,768]{1,0:T(8,128)} %get-tuple-element.363) | copy-start | bytes 9077764
  317.2 12.2 %copy-start.17 = (f32[985,768]{1,0:T(8,128)S(1)}, f32[985,768]{1,0:T(8,128)}, u32[]{:S(2)}) copy-start(f32[985,768]{1,0:T(8,128)} %reshape.821) | copy-start | bytes 9077764
  317.2 12.2 %copy-start.33 = (f32[768]{0:T(1024)S(1)}, f32[768]{0:T(1024)}, u32[]{:S(2)}) copy-start(f32[768]{0:T(1024)} %copy-done.32) | copy-start | bytes 9220
  317.2 12.2 %copy-start.35 = (f32[985]{0:T(1024)S(1)}, f32[985]{0:T(1024)}, u32[]{:S(2)}) copy-start(f32[985]{0:T(1024)} %convert_element_type.201) | copy-start | bytes 11824
  317.2 12.2 %copy-start.36 = (f32[768]{0:T(1024)S(1)}, f32[768]{0:T(1024)}, u32[]{:S(2)}) copy-start(f32[768]{0:T(1024)} %convert_element_type.197) | copy-start | bytes 9220
  329.5 11.9 %copy-start.13 = (bf16[768,768]{1,0:T(8,128)(2,1)S(1)}, bf16[768,768]{1,0:T(8,128)(2,1)}, u32[]{:S(2)}) copy-start(bf16[768,768]{1,0:T(8,128)(2,1)} %reshape.805) | copy-start | bytes 3538948
  419.5 21.0 %slice-start.3 = ((s8[6094848]{0:T(1024)(128)(4,1)}), s8[4194304]{0:T(1024)(128)(4,1)S(1)}, s32[]{:S(2)}) async-start(s8[6094848]{0:T(1024)(128)(4,1)} %bitcast.97), calls=%async_computation.9 | async-start | bytes 8388608
  422.4 18.1 %slice-start.4 = ((s8[6094848]{0:T(1024)(128)(4,1)}), s8[1900544]{0:T(1024)(128)(4,1)S(1)}, s32[]{:S(2)}) async-start(s8[6094848]{0:T(1024)(128)(4,1)} %bitcast.97), calls=%async_computation.10 | async-start | bytes 3801088
  422.4 26.9 %slice-start.5 = ((s8[6094848]{0:T(1024)(128)(4,1)}), s8[4194304]{0:T(1024)(128)(4,1)S(1)}, s32[]{:S(2)}) async-start(s8[6094848]{0:T(1024)(128)(4,1)} %bitcast.102), calls=%async_computation.11 | async-start | bytes 8388608
  433.0 16.3 %slice-start.6 = ((s8[6094848]{0:T(1024)(128)(4,1)}), s8[1900544]{0:T(1024)(128)(4,1)S(1)}, s32[]{:S(2)}) async-start(s8[6094848]{0:T(1024)(128)(4,1)} %bitcast.102), calls=%async_computation.12 | async-start | bytes 3801088
  577.9 569.5 %all-reduce.40.cloned.1.call-start = ((), (), s32[]{:S(2)}) async-start(), calls=%async_computation.5 | async-start | bytes 56623104
  (39 other events, 252.8 us)
Sparse Core Ops, SparseCore 0:
  11.1 57.0 all-gather.6
  71.1 58.9 all-gather.4
  132.9 62.3 all-gather.8
  198.1 62.3 all-gather.10
  578.0 128.7 all-reduce.37
  714.2 433.1 all-reduce.39
where the time goes:
time: 1170 us; the launch traced here: 1160 us
  waiting for transfers between devices  517 us (44%)
  local copies, waits for them, and re-layouts  277 us (24%)
  matrix products  250 us (21%)
  blocking collectives  43 us (4%)
  other arithmetic  39.4 us (3%)
  loops' own time  19.4 us (2%)
  between operations  15.4 us (1%)
    unnamed x8, waiting for transfers between devices  517 us
    unnamed x161, local copies, waits for them, and re-layouts  49.4 us
    unnamed x1, blocking collectives  43 us
    dot_general x1, matrix products, per_device(): jnp.dot(normed_post, up_w, preferred_element_type=jnp.float32) + up_b  35.7 us
    dot_general x13, matrix products, bias_rows(): jnp.einsum('rh,ar->ha', table, onehot, preferred_element_type=jnp.float32)  33.9 us
    reshape x5, local copies, waits for them, and re-layouts, unpack(): return flat[:entries].reshape(shape)  29.3 us
    dot_general x13, matrix products, add_block(): jnp.dot(upper, onehot, preferred_element_type=jnp.float32)  24 us
    dot_general x13, matrix products, add_block(): jnp.dot(lower, onehot, preferred_element_type=jnp.float32)  23.9 us
  transfers between devices with their start and end apart: 6, of which 2 were waited for; matrix products, arithmetic and copies ran while one was open for 24% of the time, Pallas kernels for 0%

commit v1 on v0

--- a/solution.py
+++ b/solution.py
@@ -1,13 +1,457 @@
+import functools
 import math
 
 import jax
 import jax.numpy as jnp
 from jax import lax
+from jax.experimental import pallas as pl
+from jax.experimental.pallas import tpu as pltpu
 from jax.sharding import PartitionSpec as P
 
 HEADS = 12
 FF = 3072
 GRID = 14
+MESH_IDS = pl.DeviceIdType.MESH
+ANY = pl.BlockSpec(memory_space=pl.ANY)
+VMEM = pl.BlockSpec(memory_space=pltpu.VMEM)
+LIMIT = 60 << 20
+
+
+class Place:
+    def __init__(self, sizes):
+        self.Y, self.A, self.B = sizes
+        self.y = lax.axis_index("dp")
+        f = lax.axis_index("fsdp")
+        self.c = f % 2
+        self.b = (f // 2) % self.B
+        self.a = f // (2 * self.B)
+
+    def dev(self, y=None, a=None, b=None, c=None):
+        y = self.y if y is None else y
+        a = self.a if a is None else a
+        b = self.b if b is None else b
+        c = self.c if c is None else c
+        return (y, (a * self.B + b) * 2 + c)
+
+    def barrier(self):
+        sem = pltpu.get_barrier_semaphore()
+        peers = [self.dev(c=1 - self.c)]
+        peers += [self.dev(a=(self.a + j) % self.A) for j in range(1, self.A)]
+        peers += [self.dev(b=(self.b + j) % self.B) for j in range(1, self.B)]
+        peers += [self.dev(y=(self.y + j) % self.Y) for j in range(1, self.Y)]
+        for peer in peers:
+            pl.semaphore_signal(sem, inc=1, device_id=peer, device_id_type=MESH_IDS)
+        pl.semaphore_wait(sem, len(peers))
+
+    def both(self, body):
+        @pl.when(self.c == 0)
+        def _():
+            body(0)
+
+        @pl.when(self.c == 1)
+        def _():
+            body(1)
+
+
+def remote(src, dst, send, recv, dev):
+    return pltpu.make_async_remote_copy(
+        src_ref=src, dst_ref=dst, send_sem=send, recv_sem=recv, device_id=dev, device_id_type=MESH_IDS
+    )
+
+
+class Gather:
+    @staticmethod
+    def sems(sizes):
+        Y, A, B = sizes
+        n = (A - 1) + (Y * B - 1) + Y * B
+        return [pltpu.SemaphoreType.DMA((n,)), pltpu.SemaphoreType.DMA((n,)), pltpu.SemaphoreType.DMA((1,))]
+
+    def __init__(self, place, shard, full, send, recv, local):
+        self.p, self.shard, self.full = place, shard, full
+        self.send, self.recv, self.local = send, recv, local
+
+    def own(self, a=None):
+        p = self.p
+        a = p.a if a is None else a
+        return self.full.at[p.y * p.A + a, p.b, p.c]
+
+    def unit(self, ry, rb, c):
+        p = self.p
+        yy = (p.y + ry) % p.Y
+        bb = (p.b + rb) % p.B
+        return self.full.at[pl.ds(yy * p.A, p.A), bb, c]
+
+    def local_copy(self):
+        return pltpu.make_async_copy(self.shard, self.own(), self.local.at[0])
+
+    def a_copy(self, j, sender):
+        p = self.p
+        dst = self.own() if sender else self.own((p.a - j) % p.A)
+        i = j - 1
+        return remote(self.shard, dst, self.send.at[i], self.recv.at[i], p.dev(a=(p.a + j) % p.A))
+
+    def unit_copy(self, core, stage, j, u, sender):
+        p = self.p
+        n1, n2 = (p.B, p.Y) if core == 0 else (p.Y, p.B)
+        if stage == 1:
+            i = j - 1
+            first, second = (0 if sender else -j), 0
+        else:
+            i = (n1 - 1) + (j - 1) * n1 + u
+            first, second = u, (0 if sender else -j)
+        ry, rb = (second, first) if core == 0 else (first, second)
+        digit_b = (core == 0) == (stage == 1)
+        dev = p.dev(b=(p.b + j) % p.B) if digit_b else p.dev(y=(p.y + j) % p.Y)
+        ref = self.unit(ry % p.Y, rb % p.B, p.c)
+        i += p.A - 1
+        return remote(ref, ref, self.send.at[i], self.recv.at[i], dev), (ry % p.Y, rb % p.B)
+
+    def twin_copy(self, ry, rb, sender):
+        p = self.p
+        i = (p.A - 1) + (p.Y * p.B - 1) + ry * p.B + rb
+        ref = self.unit(ry, rb, p.c if sender else 1 - p.c)
+        return remote(ref, ref, self.send.at[i], self.recv.at[i], p.dev(c=1 - p.c))
+
+    def start(self):
+        self.local_copy().start()
+        for j in range(1, self.p.A):
+            self.a_copy(j, True).start()
+
+    def step1(self):
+        p = self.p
+        self.local_copy().wait()
+        for j in range(1, p.A):
+            self.a_copy(j, False).wait_recv()
+
+        def body(core):
+            n1 = p.B if core == 0 else p.Y
+            for j in range(1, n1):
+                self.unit_copy(core, 1, j, 0, True)[0].start()
+
+        p.both(body)
+        self.twin_copy(0, 0, True).start()
+
+    def step2(self):
+        p = self.p
+
+        def body(core):
+            n1, n2 = (p.B, p.Y) if core == 0 else (p.Y, p.B)
+            arrived = []
+            for j in range(1, n1):
+                copy, unit = self.unit_copy(core, 1, j, 0, False)
+                copy.wait_recv()
+                arrived.append(unit)
+            for u in range(n1):
+                for j in range(1, n2):
+                    self.unit_copy(core, 2, j, u, True)[0].start()
+            for unit in arrived:
+                self.twin_copy(*unit, True).start()
+
+        p.both(body)
+
+    def step3(self):
+        p = self.p
+
+        def body(core):
+            n1, n2 = (p.B, p.Y) if core == 0 else (p.Y, p.B)
+            for u in range(n1):
+                for j in range(1, n2):
+                    copy, unit = self.unit_copy(core, 2, j, u, False)
+                    copy.wait_recv()
+                    self.twin_copy(*unit, True).start()
+
+        p.both(body)
+
+    def finish(self):
+        p = self.p
+        for ry in range(p.Y):
+            for rb in range(p.B):
+                self.twin_copy(ry, rb, False).wait_recv()
+                self.twin_copy(ry, rb, True).wait_send()
+        for j in range(1, p.A):
+            self.a_copy(j, True).wait_send()
+
+        def body(core):
+            n1, n2 = (p.B, p.Y) if core == 0 else (p.Y, p.B)
+            for j in range(1, n1):
+                self.unit_copy(core, 1, j, 0, True)[0].wait_send()
+            for u in range(n1):
+                for j in range(1, n2):
+                    self.unit_copy(core, 2, j, u, True)[0].wait_send()
+
+        p.both(body)
+
+
+class Reduce:
+    @staticmethod
+    def slots(sizes):
+        Y, A, B = sizes
+        return max((Y - 1) * B, (B - 1) * Y)
+
+    @staticmethod
+    def scratch(sizes, r, c, dtype):
+        Y, A, B = sizes
+        n = 1 + Y * B - 1 + (A - 1)
+        return [
+            pltpu.VMEM((Y * A, B, r, c), dtype),
+            pltpu.VMEM((Y * A, B, r, c), dtype),
+            pltpu.VMEM((Reduce.slots(sizes) * A, r, c), dtype),
+            pltpu.VMEM((max(Y - 1, B - 1) * A, r, c), dtype),
+            pltpu.VMEM((A - 1, r, c), dtype),
+            pltpu.SemaphoreType.DMA((n,)),
+            pltpu.SemaphoreType.DMA((n,)),
+            pltpu.SemaphoreType.DMA((1,)),
+        ]
+
+    def __init__(self, place, partial, out, own, land1, land2, land3, land4, send, recv, local):
+        self.p, self.partial, self.out = place, partial, out
+        self.own, self.land1, self.land2, self.land3, self.land4 = own, land1, land2, land3, land4
+        self.send, self.recv, self.local = send, recv, local
+
+    def twin(self):
+        p = self.p
+        return remote(
+            self.partial.at[:, :, 1 - p.c], self.land1, self.send.at[0], self.recv.at[0], p.dev(c=1 - p.c)
+        )
+
+    def local_copy(self):
+        return pltpu.make_async_copy(self.partial.at[:, :, self.p.c], self.own, self.local.at[0])
+
+    def order(self, core):
+        p = self.p
+        return (p.Y, p.B) if core == 0 else (p.B, p.Y)
+
+    def rel(self, core, first, second):
+        p = self.p
+        ry, rb = (first, second) if core == 0 else (second, first)
+        return (p.y + ry) % p.Y, (p.b + rb) % p.B
+
+    def peer(self, core, stage, j):
+        p = self.p
+        if (core == 0) == (stage == 1):
+            return p.dev(y=(p.y + j) % p.Y)
+        return p.dev(b=(p.b + j) % p.B)
+
+    def copy1(self, core, j, u):
+        p = self.p
+        n1, n2 = self.order(core)
+        yy, bb = self.rel(core, j, u)
+        slot = (j - 1) * n2 + u
+        i = 1 + slot
+        return remote(
+            self.own.at[pl.ds(yy * p.A, p.A), bb],
+            self.land2.at[pl.ds(slot * p.A, p.A)],
+            self.send.at[i],
+            self.recv.at[i],
+            self.peer(core, 1, j),
+        )
+
+    def copy2(self, core, j):
+        p = self.p
+        n1, n2 = self.order(core)
+        yy, bb = self.rel(core, 0, j)
+        i = 1 + (n1 - 1) * n2 + (j - 1)
+        return remote(
+            self.own.at[pl.ds(yy * p.A, p.A), bb],
+            self.land3.at[pl.ds((j - 1) * p.A, p.A)],
+            self.send.at[i],
+            self.recv.at[i],
+            self.peer(core, 2, j),
+        )
+
+    def copy3(self, j):
+        p = self.p
+        i = 1 + p.Y * p.B - 1 + (j - 1)
+        a = (p.a + j) % p.A
+        return remote(
+            self.own.at[p.y * p.A + a, p.b], self.land4.at[j - 1], self.send.at[i], self.recv.at[i], p.dev(a=a)
+        )
+
+    def start(self):
+        self.twin().start()
+        self.local_copy().start()
+
+    def step1(self):
+        p = self.p
+        self.local_copy().wait()
+        self.twin().wait_recv()
+
+        def add(i, _):
+            for b in range(p.B):
+                total = self.own[i, b].astype(jnp.float32) + self.land1[i, b].astype(jnp.float32)
+                self.own[i, b] = total.astype(self.own.dtype)
+            return 0
+
+        lax.fori_loop(0, p.Y * p.A, add, 0)
+
+        def body(core):
+            n1, n2 = self.order(core)
+            for j in range(1, n1):
+                for u in range(n2):
+                    self.copy1(core, j, u).start()
+
+        p.both(body)
+
+    def step2(self):
+        p = self.p
+
+        def body(core):
+            n1, n2 = self.order(core)
+            for j in range(1, n1):
+                for u in range(n2):
+                    self.copy1(core, j, u).wait_recv()
+            for u in range(n2):
+                yy, bb = self.rel(core, 0, u)
+
+                def add(i, _):
+                    total = self.own[yy * p.A + i, bb].astype(jnp.float32)
+                    for j in range(1, n1):
+                        total += self.land2[((j - 1) * n2 + u) * p.A + i].astype(jnp.float32)
+                    self.own[yy * p.A + i, bb] = total.astype(self.own.dtype)
+                    return 0
+
+                lax.fori_loop(0, p.A, add, 0)
+            for j in range(1, n2):
+                self.copy2(core, j).start()
+
+        p.both(body)
+
+    def step3(self):
+        p = self.p
+
+        def body(core):
+            n1, n2 = self.order(core)
+            for j in range(1, n2):
+                self.copy2(core, j).wait_recv()
+
+            def add(i, _):
+                total = self.own[p.y * p.A + i, p.b].astype(jnp.float32)
+                for j in range(1, n2):
+                    total += self.land3[(j - 1) * p.A + i].astype(jnp.float32)
+                self.own[p.y * p.A + i, p.b] = total.astype(self.own.dtype)
+                return 0
+
+            lax.fori_loop(0, p.A, add, 0)
+
+        p.both(body)
+        for j in range(1, p.A):
+            self.copy3(j).start()
+
+    def finish(self):
+        p = self.p
+        total = self.own[p.y * p.A + p.a, p.b].astype(jnp.float32)
+        for j in range(1, p.A):
+            self.copy3(j).wait_recv()
+            total += self.land4[j - 1].astype(jnp.float32)
+        self.out[...] = total
+        self.twin().wait_send()
+        for j in range(1, p.A):
+            self.copy3(j).wait_send()
+
+        def body(core):
+            n1, n2 = self.order(core)
+            for j in range(1, n1):
+                for u in range(n2):
+                    self.copy1(core, j, u).wait_send()
+            for j in range(1, n2):
+                self.copy2(core, j).wait_send()
+
+        p.both(body)
+
+
+def gather_kernel(sizes, n, *refs):
+    shards, fulls, sems = refs[:n], refs[n : 2 * n], refs[2 * n :]
+    place = Place(sizes)
+    place.barrier()
+    gathers = [Gather(place, shards[k], fulls[k], *sems[3 * k : 3 * k + 3]) for k in range(n)]
+    for g in gathers:
+        g.start()
+    for g in gathers:
+        g.step1()
+    for g in gathers:
+        g.step2()
+    for g in gathers:
+        g.step3()
+    for g in gathers:
+        g.finish()
+
+
+def gather_call(sizes, shards, collective_id):
+    Y, A, B = sizes
+    n = len(shards)
+    shapes = [jax.ShapeDtypeStruct((Y * A, B, 2, *s.shape), s.dtype) for s in shards]
+    return pl.pallas_call(
+        functools.partial(gather_kernel, sizes, n),
+        out_shape=shapes,
+        in_specs=[ANY] * n,
+        out_specs=[ANY] * n,
+        scratch_shapes=[s for _ in range(n) for s in Gather.sems(sizes)],
+        compiler_params=pltpu.CompilerParams(
+            collective_id=collective_id, has_side_effects=True, vmem_limit_bytes=LIMIT
+        ),
+        name="gather",
+    )(*shards)
+
+
+def reduce_kernel(sizes, n, *refs):
+    partials, outs, scratch = refs[:n], refs[n : 2 * n], refs[2 * n :]
+    place = Place(sizes)
+    place.barrier()
+    sums = [Reduce(place, partials[k], outs[k], *scratch[8 * k : 8 * k + 8]) for k in range(n)]
+    for s in sums:
+        s.start()
+    for s in sums:
+        s.step1()
+    for s in sums:
+        s.step2()
+    for s in sums:
+        s.step3()
+    for s in sums:
+        s.finish()
+
+
+def reduce_call(sizes, partials, collective_id):
+    Y, A, B = sizes
+    n = len(partials)
+    partials = [x.reshape(Y * A, B, 2, *x.shape[1:]) for x in partials]
+    shapes = [jax.ShapeDtypeStruct(x.shape[3:], jnp.float32) for x in partials]
+    return pl.pallas_call(
+        functools.partial(reduce_kernel, sizes, n),
+        out_shape=shapes,
+        in_specs=[ANY] * n,
+        out_specs=[VMEM] * n,
+        scratch_shapes=[
+            s for x in partials for s in Reduce.scratch(sizes, x.shape[3], x.shape[4], x.dtype)
+        ],
+        compiler_params=pltpu.CompilerParams(
+            collective_id=collective_id, has_side_effects=True, vmem_limit_bytes=LIMIT
+        ),
+        name="reduce",
+    )(*partials)
+
+
+def mesh_sizes(dp, fsdp):
+    chips = fsdp // 2
+    across = math.gcd(chips, 4)
+    return (dp, across, chips // across)
+
+
+def block_shape(entries, width):
+    rows = entries // width
+    return (rows, width) if rows % 8 == 0 else (entries // 128, 128)
+
+
+TILE = 16
+
+
+def pack_small(vectors, hidden, table):
+    lanes = 128
+    rows = [jnp.pad(v, (0, lanes - v.shape[0])) for v in vectors]
+    rows.append(jnp.pad(hidden, (0, lanes - hidden.shape[0])))
+    table_rows = -(-table.shape[0] // lanes)
+    rows.append(jnp.pad(table, (0, table_rows * lanes - table.shape[0])))
+    flat = jnp.concatenate(rows)
+    return jnp.pad(flat, (0, TILE * lanes - flat.shape[0])).reshape(TILE, lanes)
 
 
 norm_eps = 1e-06
@@ -67,35 +511,6 @@
     return (
         0.5 * (1.0 + lax.erf(values * 0.7071067811865476))
         + values * jnp.exp(-0.5 * values * values) * 0.3989422804014327
-    )
-
-
-def attn_unpack(full, model_dim, table_rows, heads):
-    wide = [piece.astype(jnp.float32) for piece in full]
-    return (
-        wide[0],
-        wide[1],
-        wide[2],
-        unpack(full[3], (model_dim, 3 * model_dim)),
-        wide[4],
-        wide[5],
-        unpack(full[6], (table_rows, heads)),
-        unpack(full[7], (model_dim, model_dim)),
-        wide[8],
-        wide[9],
-    )
-
-
-def mlp_unpack(full, model_dim, hidden_dim):
-    wide = [piece.astype(jnp.float32) for piece in full]
-    return (
-        wide[0],
-        wide[1],
-        unpack(full[2], (model_dim, hidden_dim)),
-        wide[3],
-        unpack(full[4], (hidden_dim, model_dim)),
-        wide[5],
-        wide[6],
     )
 
 
@@ -131,34 +546,26 @@
     padded_rows = block_count * block_rows
     four_dims = (images, seq_len, heads, head_dim)
     total_devices = lax.axis_size(("dp", "fsdp"))
-    attn_shards = (
-        mask_token,
-        pre_gain,
-        pre_shift,
-        qkv_weight,
-        query_bias,
-        value_bias,
-        rel_table,
-        out_weight,
-        out_bias,
-        attn_scale,
-    )
-    mlp_shards = (post_gain, post_shift, up_weight, up_bias, down_weight, down_bias, mlp_scale)
-    attn_full = (
-        lax.all_gather(mask_token, ("dp", "fsdp"), axis=0, tiled=True),
-        lax.all_gather(pre_gain, ("dp", "fsdp"), axis=0, tiled=True),
-        lax.all_gather(pre_shift, ("dp", "fsdp"), axis=0, tiled=True),
-        lax.all_gather(qkv_weight, ("dp", "fsdp"), axis=0, tiled=True),
-        lax.all_gather(query_bias, ("dp", "fsdp"), axis=0, tiled=True),
-        lax.all_gather(value_bias, ("dp", "fsdp"), axis=0, tiled=True),
-        lax.all_gather(rel_table, ("dp", "fsdp"), axis=0, tiled=True),
-        lax.all_gather(out_weight, ("dp", "fsdp"), axis=0, tiled=True),
-        lax.all_gather(out_bias, ("dp", "fsdp"), axis=0, tiled=True),
-        lax.all_gather(attn_scale, ("dp", "fsdp"), axis=0, tiled=True),
-    )
-    token_fill, pre_g, pre_s, qkv_w, query_b, value_b, table, out_w, out_b, attn_g = attn_unpack(
-        attn_full, model_dim, table_rows, heads
-    )
+    sizes = mesh_sizes(lax.axis_size("dp"), lax.axis_size("fsdp"))
+    vec_shards = (
+        mask_token, pre_gain, pre_shift, query_bias, value_bias, out_bias, attn_scale,
+        post_gain, post_shift, down_bias, mlp_scale,
+    )
+    small = pack_small(vec_shards, up_bias, rel_table)
+    widths = (3 * model_dim, model_dim, hidden_dim, model_dim)
+    mats = (qkv_weight, out_weight, up_weight, down_weight)
+    blocks = [m.reshape(block_shape(m.shape[0], w)) for m, w in zip(mats, widths)]
+    small_full, *mats_full = gather_call(sizes, [small] + blocks, 0)
+    qkv_w, out_w, up_w, down_w = [m.reshape(-1, w) for m, w in zip(mats_full, widths)]
+    rows_full = small_full.reshape(total_devices, TILE, 128)
+    per_vec = mask_token.shape[0]
+    vectors = [rows_full[:, i, :per_vec].reshape(-1).astype(jnp.float32) for i in range(11)]
+    (
+        token_fill, pre_g, pre_s, query_b, value_b, out_b, attn_g, post_g, post_s, down_b, mlp_g,
+    ) = vectors
+    up_b = rows_full[:, 11, : up_bias.shape[0]].reshape(-1).astype(jnp.float32)
+    table = rows_full[:, 12:].reshape(total_devices, -1)[:, : rel_table.shape[0]].reshape(-1)
+    table = table[: table_rows * heads].reshape(table_rows, heads)
     masked = patch_mask.reshape(-1, 1) == 1
     token_rows = patches.reshape(-1, model_dim).astype(jnp.float32)
     initial = jnp.where(masked, token_fill[None, :], token_rows)
@@ -196,16 +603,6 @@
     attended = attended.reshape(-1, model_dim).astype(jnp.bfloat16)
     branch = jnp.dot(attended, out_w, preferred_element_type=jnp.float32) + out_b
     middle = initial + attn_g * branch
-    mlp_full = (
-        lax.all_gather(post_gain, ("dp", "fsdp"), axis=0, tiled=True),
-        lax.all_gather(post_shift, ("dp", "fsdp"), axis=0, tiled=True),
-        lax.all_gather(up_weight, ("dp", "fsdp"), axis=0, tiled=True),
-        lax.all_gather(up_bias, ("dp", "fsdp"), axis=0, tiled=True),
-        lax.all_gather(down_weight, ("dp", "fsdp"), axis=0, tiled=True),
-        lax.all_gather(down_bias, ("dp", "fsdp"), axis=0, tiled=True),
-        lax.all_gather(mlp_scale, ("dp", "fsdp"), axis=0, tiled=True),
-    )
-    post_g, post_s, up_w, up_b, down_w, down_b, mlp_g = mlp_unpack(mlp_full, model_dim, hidden_dim)
     normal_post, inverse_post = normalize(middle)
     normed_post = (normal_post * post_g + post_s).astype(jnp.bfloat16)
     up_rows = jnp.dot(normed_post, up_w, preferred_element_type=jnp.float32) + up_b
@@ -213,18 +610,6 @@
     down_rows = jnp.dot(hidden, down_w, preferred_element_type=jnp.float32) + down_b
     result = middle + mlp_g * down_rows
     layer_out = result.astype(jnp.bfloat16).reshape(patches.shape)
-    mlp_second = (
-        lax.all_gather(post_gain, ("dp", "fsdp"), axis=0, tiled=True),
-        lax.all_gather(post_shift, ("dp", "fsdp"), axis=0, tiled=True),
-        lax.all_gather(up_weight, ("dp", "fsdp"), axis=0, tiled=True),
-        lax.all_gather(up_bias, ("dp", "fsdp"), axis=0, tiled=True),
-        lax.all_gather(down_weight, ("dp", "fsdp"), axis=0, tiled=True),
-        lax.all_gather(down_bias, ("dp", "fsdp"), axis=0, tiled=True),
-        lax.all_gather(mlp_scale, ("dp", "fsdp"), axis=0, tiled=True),
-    )
-    post_g, post_s, up_w, up_b, down_w, down_b, mlp_g = mlp_unpack(
-        mlp_second, model_dim, hidden_dim
-    )
     grad_out = cotangent.reshape(-1, model_dim).astype(jnp.float32) * masked.astype(jnp.float32)
     mlp_scale_grad = jnp.sum(grad_out * down_rows, axis=0)
     grad_down_rows = mlp_g * grad_out
@@ -244,42 +629,6 @@
     post_gain_grad = jnp.sum(grad_normed_post * normal_post, axis=0)
     post_shift_grad = jnp.sum(grad_normed_post, axis=0)
     grad_middle = grad_out + norm_back(grad_normed_post, normal_post, inverse_post, post_g)
-    mlp_lists = (
-        post_gain_grad,
-        post_shift_grad,
-        up_weight_grad,
-        up_bias_grad,
-        down_weight_grad,
-        down_bias_grad,
-        mlp_scale_grad,
-    )
-    mlp_flat = [
-        pad_flat(grad, shard.shape[0] * total_devices) for grad, shard in zip(mlp_lists, mlp_shards)
-    ]
-    mlp_owned = (
-        lax.psum_scatter(mlp_flat[0], ("dp", "fsdp"), scatter_dimension=0, tiled=True),
-        lax.psum_scatter(mlp_flat[1], ("dp", "fsdp"), scatter_dimension=0, tiled=True),
-        lax.psum_scatter(mlp_flat[2], ("dp", "fsdp"), scatter_dimension=0, tiled=True),
-        lax.psum_scatter(mlp_flat[3], ("dp", "fsdp"), scatter_dimension=0, tiled=True),
-        lax.psum_scatter(mlp_flat[4], ("dp", "fsdp"), scatter_dimension=0, tiled=True),
-        lax.psum_scatter(mlp_flat[5], ("dp", "fsdp"), scatter_dimension=0, tiled=True),
-        lax.psum_scatter(mlp_flat[6], ("dp", "fsdp"), scatter_dimension=0, tiled=True),
-    )
-    attn_second = (
-        lax.all_gather(mask_token, ("dp", "fsdp"), axis=0, tiled=True),
-        lax.all_gather(pre_gain, ("dp", "fsdp"), axis=0, tiled=True),
-        lax.all_gather(pre_shift, ("dp", "fsdp"), axis=0, tiled=True),
-        lax.all_gather(qkv_weight, ("dp", "fsdp"), axis=0, tiled=True),
-        lax.all_gather(query_bias, ("dp", "fsdp"), axis=0, tiled=True),
-        lax.all_gather(value_bias, ("dp", "fsdp"), axis=0, tiled=True),
-        lax.all_gather(rel_table, ("dp", "fsdp"), axis=0, tiled=True),
-        lax.all_gather(out_weight, ("dp", "fsdp"), axis=0, tiled=True),
-        lax.all_gather(out_bias, ("dp", "fsdp"), axis=0, tiled=True),
-        lax.all_gather(attn_scale, ("dp", "fsdp"), axis=0, tiled=True),
-    )
-    token_fill, pre_g, pre_s, qkv_w, query_b, value_b, table, out_w, out_b, attn_g = attn_unpack(
-        attn_second, model_dim, table_rows, heads
-    )
     attn_scale_grad = jnp.sum(grad_middle * branch, axis=0)
     grad_branch_rows = attn_g * grad_middle
     out_bias_grad = jnp.sum(grad_branch_rows, axis=0)
@@ -352,54 +701,39 @@
         (jnp.arange(block_count, dtype=jnp.int32), bias_grid),
     )
     table_grad = jnp.transpose(table_grad_t)
-    attn_lists = (
-        mask_token_grad,
-        pre_gain_grad,
-        pre_shift_grad,
-        qkv_weight_grad,
-        query_bias_grad,
-        value_bias_grad,
-        table_grad,
-        out_weight_grad,
-        out_bias_grad,
-        attn_scale_grad,
-    )
-    attn_flat = [
-        pad_flat(grad, shard.shape[0] * total_devices)
-        for grad, shard in zip(attn_lists, attn_shards)
+    vec_grads = (
+        mask_token_grad, pre_gain_grad, pre_shift_grad, query_bias_grad, value_bias_grad,
+        out_bias_grad, attn_scale_grad, post_gain_grad, post_shift_grad, down_bias_grad,
+        mlp_scale_grad,
+    )
+    table_flat = pad_flat(table_grad, rel_table.shape[0] * total_devices)
+
+    def lanes(value, count):
+        value = value.reshape(total_devices, -1)
+        return jnp.pad(value, ((0, 0), (0, count - value.shape[1])))
+
+    small_grad = jnp.concatenate(
+        [lanes(v, 128) for v in vec_grads]
+        + [lanes(up_bias_grad, 128), lanes(table_flat, (TILE - 12) * 128)],
+        axis=1,
+    ).reshape(total_devices, TILE, 128)
+    mat_grads = (qkv_weight_grad, out_weight_grad, up_weight_grad, down_weight_grad)
+    partials = [
+        g.astype(jnp.bfloat16).reshape(total_devices, *b.shape) for g, b in zip(mat_grads, blocks)
     ]
-    attn_owned = (
-        lax.psum_scatter(attn_flat[0], ("dp", "fsdp"), scatter_dimension=0, tiled=True),
-        lax.psum_scatter(attn_flat[1], ("dp", "fsdp"), scatter_dimension=0, tiled=True),
-        lax.psum_scatter(attn_flat[2], ("dp", "fsdp"), scatter_dimension=0, tiled=True),
-        lax.psum_scatter(attn_flat[3], ("dp", "fsdp"), scatter_dimension=0, tiled=True),
-        lax.psum_scatter(attn_flat[4], ("dp", "fsdp"), scatter_dimension=0, tiled=True),
-        lax.psum_scatter(attn_flat[5], ("dp", "fsdp"), scatter_dimension=0, tiled=True),
-        lax.psum_scatter(attn_flat[6], ("dp", "fsdp"), scatter_dimension=0, tiled=True),
-        lax.psum_scatter(attn_flat[7], ("dp", "fsdp"), scatter_dimension=0, tiled=True),
-        lax.psum_scatter(attn_flat[8], ("dp", "fsdp"), scatter_dimension=0, tiled=True),
-        lax.psum_scatter(attn_flat[9], ("dp", "fsdp"), scatter_dimension=0, tiled=True),
-    )
+    *mat_own, small_own = reduce_call(sizes, partials + [small_grad], 1)
+    qkv_o, out_o, up_o, down_o = [m.reshape(-1) for m in mat_own]
+    vec_o = [small_own[i, :per_vec] for i in range(11)]
+    up_bias_o = small_own[11, : up_bias.shape[0]]
+    table_o = small_own[12:].reshape(-1)[: rel_table.shape[0]]
+    (
+        token_o, pre_gain_o, pre_shift_o, query_bias_o, value_bias_o, out_bias_o, attn_scale_o,
+        post_gain_o, post_shift_o, down_bias_o, mlp_scale_o,
+    ) = vec_o
     return (
-        layer_out,
-        patch_grad,
-        attn_owned[0],
-        attn_owned[1],
-        attn_owned[2],
-        attn_owned[3],
-        attn_owned[4],
-        attn_owned[5],
-        attn_owned[6],
-        attn_owned[7],
-        attn_owned[8],
-        attn_owned[9],
-        mlp_owned[0],
-        mlp_owned[1],
-        mlp_owned[2],
-        mlp_owned[3],
-        mlp_owned[4],
-        mlp_owned[5],
-        mlp_owned[6],
+        layer_out, patch_grad, token_o, pre_gain_o, pre_shift_o, qkv_o, query_bias_o, value_bias_o,
+        table_o, out_o, out_bias_o, attn_scale_o, post_gain_o, post_shift_o, up_o, up_bias_o,
+        down_o, down_bias_o, mlp_scale_o,
     )
 
 

time: 1170 us -> 754 us (0.64)
  waiting for transfers between devices: 517 us -> 0 us
  Pallas kernels: 0 us -> 198 us
  local copies, waits for them, and re-layouts: 277 us -> 226 us
  blocking collectives: 43 us -> 0 us
  between operations: 15.4 us -> 1.84 us
    unnamed x8 -> x0, waiting for transfers between devices: 517 us -> none
    pallas_call x0 -> x2, Pallas kernels: none -> 198 us  [the longest x1 104 us: reduce_call(): pl.pallas_call(functools.partial(reduce_kernel, sizes, n), out_shape=shap...]
    unnamed x1 -> x0, blocking collectives: 43 us -> none
    unnamed x161 -> x90, local copies, waits for them, and re-layouts: 49.4 us -> 15.1 us
    reshape x4 -> x1, local copies, waits for them, and re-layouts: 20.7 us -> 0.27 us  [pad_flat(): flat = values.reshape(-1)]
    reshape x5 -> x24, local copies, waits for them, and re-layouts: 29.3 us -> 15 us  [the longest x4 6.61 us: per_device(): m.reshape(block_shape(m.shape[0], w))]
  transfers between devices with their start and end apart: 6 -> 0, of which waited for: 2 -> 0; matrix products, arithmetic and copies ran while one was open for 24% -> 0% of each run, Pallas kernels for 0% -> 0%
where the time goes in v1:
time: 754 us; the launch traced here: 743 us
  matrix products  258 us (34%)
  local copies, waits for them, and re-layouts  226 us (30%)
  Pallas kernels  198 us (26%)
  other arithmetic  41.6 us (6%)
  loops' own time  19.1 us (3%)
    pallas_call x1, Pallas kernels, reduce_call(): pl.pallas_call(functools.partial(reduce_kernel, sizes, n), out_shape=shap...  104 us
    pallas_call x1, Pallas kernels, gather_call(): pl.pallas_call(functools.partial(gather_kernel, sizes, n), out_shape=shap...  93.2 us
    dot_general x1, matrix products, per_device(): jnp.dot(normed_post, up_w, preferred_element_type=jnp.float32) + up_b  35.8 us
    dot_general x13, matrix products, bias_rows(): jnp.einsum('rh,ar->ha', table, onehot, preferred_element_type=jnp.float32)  34 us
    dot_general x13, matrix products, add_block(): jnp.dot(upper, onehot, preferred_element_type=jnp.float32)  24 us
    dot_general x13, matrix products, add_block(): jnp.dot(lower, onehot, preferred_element_type=jnp.float32)  23.9 us
    dynamic_slice x13, local copies, waits for them, and re-layouts, per_device(): lax.scan(add_block, jnp.zeros((heads, table_rows), jnp.float32), (jnp.ara...  18.2 us
    dynamic_slice x26, local copies, waits for them, and re-layouts, per_device(): bias_pieces = lax.map(bias_rows, jnp.arange(block_count, dtype=jnp.int32))  15.2 us

profile of v1, /device:TPU:0, one launch (start us, length us, event | category | flops | bytes accessed | tf_op | source)
XLA Modules:
  0.0 743.3 jit_solution(6599004457482131222)
XLA Ops:
  18.8 93.2 %gather.1 = (bf16[8,2,2,16,128]{4,3,2,1,0:T(8,128)(2,1)}, bf16[8,2,2,24,2304]{4,3,2,1,0:T(8,128)(2,1)}, bf16[8,2,2,24,768]{4,3,2,1,0:T(8,128)(2,1)}, bf16[8,2,2,...) custom-call(bf16[16,128]{1,0:T(8,128)(2,1)} %pad_bitcast_fusion.refs_0_, bf16[24,2304]{1,0:T(8,128)(2,1)} %reshape.940.refs_1_, ...), custom_call_target="tpu_custom_call" | custom-call | tf_op jit(solution)/shard_map/gather/pallas_call | solution.py:383
  121.7 8.2 %fusion.75 = f32[985,2304]{1,0:T(8,128)} fusion(bf16[985,768]{1,0:T(8,128)(2,1)S(1)} %convert_element_type.311, bf16[768,2304]{1,0:T(8,128)(2,1)} %bitcast.183), kind=kOutput, calls=%fused_computation.202 | convolution fusion | flops 3485859840 | bytes 14129664 | tf_op jit(solution)/shard_map/dot_general | solution.py:574
  138.8 6.0 copy.102
  146.4 66.2 %while.31 = (s32[]{:T(128)}, f32[13,12,3152]{2,1,0:T(8,128)}, s32[13]{0:T(128)S(1)}, bf16[732,12]{0,1:T(8,128)(2,1)S(1)}, s32[]{:T(128)}, /*index=5*/s32[1]{0:T(128)}) while((s32[]{:T(128)}, f32[13,12,3152]{2,1,0:T(8,128)}, s32[13]{0:T(128)S(1)}, bf16[732,12]{0,1:T(8,128)(2,1)S(1)}, s32[]{:T(128)}, /*index=5*/s32[1]{0:T(128)}) %tuple.146), condition=%wide.region_3.4_spmd, body=%wide.region_2.3_spmd.sunk | while | flops 57719896 | bytes 491115 | solution.py:583
  227.5 6.0 copy.97
  242.5 6.4 copy.98
  248.9 8.5 %add_reduce_fusion = (f32[5,12,197]{2,1,0:T(8,128)S(1)}, f32[5,12,197,197]{2,3,1,0:T(8,128)}) fusion(f32[12,197,197]{1,2,0:T(8,128)S(1)} %copy.101, bf16[5,197,12,64]{1,3,2,0:T(8,128)(2,1)} %copy.97, bf16[5,197,12,64]{1,3,2,0:T(8,128)(2,1)} %copy.98), kind=kOutput, calls=%fused_computation.80 | convolution fusion | flops 302698368 | bytes 14250192 | tf_op jit(solution)/shard_map/ishd,ithd->ihst/dot_general | solution.py:589
  257.4 7.6 %fusion.43 = f32[5,12,197]{2,1,0:T(8,128)S(1)} fusion(f32[5,12,197,197]{2,3,1,0:T(8,128)} %get-tuple-element.374, f32[5,12,197]{2,1,0:T(8,128)S(1)} %get-tuple-element.373, f32[12,197,197]{1,2,0:T(8,128)S(1)} %copy.101), kind=kLoop, calls=%fused_computation.79 | loop fusion | flops 6973800 | bytes 11271552 | tf_op jit(solution)/shard_map/reduce_sum | solution.py:594
  265.0 7.4 convert_bitcast_fusion.1
  281.2 6.1 fusion.72
  290.6 35.8 %fusion.30 = (bf16[985,3072]{1,0:T(8,128)(2,1)}, f32[985,3072]{1,0:T(8,128)}) fusion(f32[3072]{0:T(1024)S(1)} %reshape.994, bf16[768,3072]{1,0:T(8,128)(2,1)} %bitcast.181, f32[985,768]{1,0:T(8,128)} %copy-done.6, f32[768]{0:T(1024)S(1)} %reshape.993, f32[768]{0:T(1024)S(1)} %reshape.992, f32[985]{0:T(1024)S(1)} %add_rsqrt_fusion.1, ...), kind=kOutput, calls=%fused_computation.58 | convolution fusion | flops 4851306496 | bytes 25926344 | tf_op jit(solution)/shard_map/dot_general | solution.py:608
  332.4 12.2 %fusion.74 = (f32[3072]{0:T(1024)S(1)}, bf16[985,3072]{1,0:T(8,128)(2,1)S(1)}) fusion(f32[985,3072]{1,0:T(8,128)} %get-tuple-element.378, f32[3072]{0:T(1024)S(1)} %reshape.994, bf16[985,768]{1,0:T(8,128)(2,1)} %convert_element_type.343, bf16[3072,768]{1,0:T(8,128)(2,1)} %bitcast.179), kind=kOutput, calls=%fused_computation.201 | convolution fusion | flops 4684121088 | bytes 24411648 | tf_op jit(solution)/shard_map/rb,ab->ra/dot_general | solution.py:621
  344.7 11.5 %multiply_reduce_fusion.3 = (f32[768]{0:T(1024)S(1)}, f32[985]{0:T(1024)S(1)}, f32[985]{0:T(1024)S(1)}, f32[768]{0:T(1024)S(1)}, f32[985,768]{1,0:T(8,128)}) fusion(f32[985,768]{1,0:T(8,128)S(1)} %copy-done.7, f32[985]{0:T(1024)S(1)} %add_rsqrt_fusion.1, f32[985]{0:T(1024)S(1)} %broadcast_multiply_fusion.5, f32[768]{0:T(1024)S(1)} %reshape.992, ...), kind=kOutput, calls=%fused_computation.107 | convolution fusion | flops 4654619648 | bytes 16847248 | tf_op jit(solution)/shard_map/rb,ab->ra/dot_general | solution.py:628
  359.8 13.5 %multiply_reduce_fusion.4 = (f32[768]{0:T(1024)S(1)}, f32[768]{0:T(1024)S(1)}, f32[985,768]{1,0:T(8,128)}, f32[768]{0:T(1024)S(1)}, bf16[985,768]{1,0:T(8,128)(2,1)}) fusion(f32[985,768]{1,0:T(8,128)} %get-tuple-element.375, f32[768]{0:T(1024)S(1)} %reshape.990, f32[768]{0:T(1024)S(1)} %reshape.985, f32[985]{0:T(1024)S(1)} %broadcast_multiply_fusion.3, ...), kind=kOutput, calls=%fused_computation.108 | convolution fusion | flops 4662941696 | bytes 27457268 | tf_op jit(solution)/shard_map/dot_general | solution.py:610
  386.9 6.4 copy.111
  393.4 13.2 %multiply_reduce_fusion = (f32[5,12,197]{2,1,0:T(8,128)S(1)}, f32[5,12,197,197]{2,3,1,0:T(8,128)}) fusion(f32[5,12,197,197]{2,3,1,0:T(8,128)} %get-tuple-element.374, f32[5,12,197]{2,1,0:T(8,128)S(1)} %log_add_fusion, f32[12,197,197]{1,2,0:T(8,128)S(1)} %copy.101, bf16[5,197,12,64]{1,3,2,0:T(8,128)(2,1)} %copy.111, bf16[5,197,12,64]{1,3,2,0:T(8,128)(2,1)} %copy.102), kind=kOutput, calls=%fused_computation.52 | convolution fusion | flops 307355456 | bytes 23611632 | tf_op jit(solution)/shard_map/ishd,ithd->ihst/dot_general | solution.py:646
  406.6 11.6 %fusion.70 = (f32[12,197,197]{1,2,0:T(8,128)}, bf16[5,12,197,197]{2,3,1,0:T(8,128)(2,1)S(1)}) fusion(f32[5,12,197,197]{2,3,1,0:T(8,128)} %get-tuple-element.380, f32[5,12,197]{2,1,0:T(8,128)S(1)} %get-tuple-element.379, f32[5,12,197]{2,1,0:T(8,128)S(1)} %log_add_fusion, f32[5,12,197,197]{2,3,1,0:T(8,128)} %get-tuple-element.374, f32[12,197,197]{1,2,0:T(8,128)S(1)} %copy.101), kind=kLoop, calls=%fused_computation.197 | loop fusion | flops 13505532 | bytes 27105624 | tf_op jit(solution)/shard_map/reduce_sum | solution.py:657
  450.3 8.6 %bitcast_convert_fusion = (bf16[5,197,12,64]{1,3,2,0:T(8,128)(2,1)S(1)}, f32[5,12,64,197]{3,2,1,0:T(8,128)}) fusion(bf16[5,197,12,64]{1,3,2,0:T(8,128)(2,1)S(1)} %copy-done.5, f32[5,12,197,197]{2,3,1,0:T(8,128)} %get-tuple-element.374, f32[5,12,197]{2,1,0:T(8,128)S(1)} %log_add_fusion, f32[12,197,197]{1,2,0:T(8,128)S(1)} %copy.101), kind=kOutput, calls=%fused_computation.90 | convolution fusion | flops 305795232 | bytes 17276112 | tf_op jit(solution)/shard_map/ihst,ishd->ithd/dot_general | solution.py:649
  470.4 8.4 %multiply_reduce_fusion.5 = (f32[768]{0:T(1024)S(1)}, f32[985]{0:T(1024)S(1)}, f32[985]{0:T(1024)S(1)}, f32[768]{0:T(1024)S(1)}, f32[985,768]{1,0:T(8,128)S(1)}) fusion(f32[985]{0:T(1024)S(1)} %rsqrt.22, f32[985]{0:T(1024)S(1)} %div.111, f32[985,768]{1,0:T(8,128)S(1)} %copy-done.1, f32[768]{0:T(1024)S(1)} %copy-done.16, pred[985]{0:T(1024)(128)(4,1)S(1)} %eq.137, ...), kind=kOutput, calls=%fused_computation.109 | convolution fusion | flops 3493421056 | bytes 14158697 | tf_op jit(solution)/shard_map/rb,ab->ra/dot_general | solution.py:677
  485.3 8.8 %convolution_convert_fusion.2 = bf16[768,2304]{1,0:T(8,128)(2,1)} fusion(bf16[985,2304]{0,1:T(8,128)(2,1)} %constant_dynamic-update-slice_fusion, f32[768]{0:T(1024)S(1)} %copy-done.25, f32[768]{0:T(1024)S(1)} %copy-done.22, f32[985,768]{1,0:T(8,128)S(1)} %copy-done.1, f32[985]{0:T(1024)S(1)} %div.111, f32[985]{0:T(1024)S(1)} %rsqrt.22, ...), kind=kOutput, calls=%fused_computation.88 | convolution fusion | flops 3492168192 | bytes 11121825 | tf_op jit(solution)/shard_map/ra,rb->ab/dot_general | solution.py:674
  496.5 10.0 %convolution_convert_fusion.1 = bf16[768,3072]{1,0:T(8,128)(2,1)} fusion(bf16[985,3072]{1,0:T(8,128)(2,1)} %copy-done.27, f32[985,768]{1,0:T(8,128)S(1)} %copy-done.8, f32[768]{0:T(1024)S(1)} %reshape.993, f32[768]{0:T(1024)S(1)} %reshape.992, f32[985]{0:T(1024)S(1)} %add_rsqrt_fusion.1, f32[985]{0:T(1024)S(1)} %broadcast_multiply_fusion.5), kind=kOutput, calls=%fused_computation.87 | convolution fusion | flops 4653955072 | bytes 13810376 | tf_op jit(solution)/shard_map/ra,rb->ab/dot_general | solution.py:625
  506.5 7.7 %convolution_convert_fusion = bf16[3072,768]{1,0:T(8,128)(2,1)} fusion(bf16[985,3072]{1,0:T(8,128)(2,1)S(1)} %bitcast.186, f32[985,768]{1,0:T(8,128)S(1)} %copy-done.14, f32[985]{0:T(1024)S(1)} %convert_element_type.339, f32[768]{0:T(1024)S(1)} %reshape.991), kind=kOutput, calls=%fused_computation.86 | convolution fusion | flops 4652441600 | bytes 13803364 | tf_op jit(solution)/shard_map/ra,rb->ab/dot_general | solution.py:618
  527.9 98.7 %while.32 = (s32[]{:T(128)}, f32[12,732]{1,0:T(8,128)S(1)}, f32[13,12,3152]{2,0,1:T(8,128)}, s32[13]{0:T(128)S(1)}, s32[]{:T(128)}, /*index=5*/s32[1]{0:T(128)}, s32[]{:T(128)}) while((s32[]{:T(128)}, f32[12,732]{1,0:T(8,128)S(1)}, f32[13,12,3152]{2,0,1:T(8,128)}, s32[13]{0:T(128)S(1)}, s32[]{:T(128)}, /*index=5*/s32[1]{0:T(128)}, ...), condition=%wide.region_27.28_spmd.clone, body=%wide.region_26.27_spmd.clone.sunk | while | flops 115579144 | bytes 1027101 | solution.py:698
  628.0 104.4 %reduce.26 = (f32[24,2304]{1,0:T(8,128)}, f32[24,768]{1,0:T(8,128)}, f32[24,3072]{1,0:T(8,128)}, f32[96,768]{1,0:T(8,128)}, f32[16,128]{1,0:T(8,128)}) custom-call(bf16[8,2,2,24,2304]{4,3,2,1,0:T(8,128)(2,1)} %bitcast.163, bf16[8,2,2,24,768]{4,3,2,1,0:T(8,128)(2,1)} %bitcast.166, bf16[8,2,2,24,3072]{4,3,2,1,0:T(8,128)(2,1)} %bitcast.160, ...), custom_call_target="tpu_custom_call" | custom-call | tf_op jit(solution)/shard_map/reduce/pallas_call | solution.py:418
  (815 shorter events, 320.8 us)
Async XLA Ops:
  15.4 102.0 %copy-start.26 = (s32[5,197]{1,0:T(8,128)S(1)}, s32[5,197]{1,0:T(8,128)}, u32[]{:S(2)}) copy-start(s32[5,197]{1,0:T(8,128)} %param.25) | copy-start | bytes 11824
  17.0 101.3 %copy-start.2 = (bf16[5,197,768]{2,1,0:T(8,128)(2,1)S(1)}, bf16[5,197,768]{2,1,0:T(8,128)(2,1)}, u32[]{:S(2)}) copy-start(bf16[5,197,768]{2,1,0:T(8,128)(2,1)} %param.24) | copy-start | bytes 4538884
  117.4 163.8 %copy-start.15 = (f32[768]{0:T(1024)}, f32[768]{0:T(1024)S(1)}, u32[]{:S(2)}) copy-start(f32[768]{0:T(1024)S(1)} %reshape.983) | copy-start | bytes 9220
  118.2 3.0 copy-start.24
  118.3 2.9 copy-start.21
  257.4 7.6 %copy-start.10 = (bf16[5,197,12,64]{1,3,2,0:T(8,128)(2,1)S(1)}, bf16[5,197,12,64]{1,3,2,0:T(8,128)(2,1)}, u32[]{:S(2)}) copy-start(bf16[5,197,12,64]{1,3,2,0:T(8,128)(2,1)} %copy.102) | copy-start | bytes 4538884
  290.6 35.9 %copy-start.23 = (f32[5,197]{1,0:T(8,128)S(1)}, f32[5,197]{1,0:T(8,128)}, u32[]{:S(2)}) copy-start(f32[5,197]{1,0:T(8,128)} %get-tuple-element.333) | copy-start | bytes 11824
  332.4 12.3 %copy-start.7 = (f32[985,768]{1,0:T(8,128)S(1)}, f32[985,768]{1,0:T(8,128)}, u32[]{:S(2)}) copy-start(f32[985,768]{1,0:T(8,128)} %copy-done.6) | copy-start | bytes 9077764
  344.7 11.5 %copy-start.27 = (bf16[985,3072]{1,0:T(8,128)(2,1)}, bf16[985,3072]{1,0:T(8,128)(2,1)S(1)}, u32[]{:S(2)}) copy-start(bf16[985,3072]{1,0:T(8,128)(2,1)S(1)} %get-tuple-element.387) | copy-start | bytes 18155524
  373.3 3.0 copy-start.20
  373.3 3.0 copy-start.18
  406.6 11.6 %copy-start.3 = (bf16[5,197,12,64]{1,3,2,0:T(8,128)(2,1)S(1)}, bf16[5,197,12,64]{1,3,2,0:T(8,128)(2,1)}, u32[]{:S(2)}) copy-start(bf16[5,197,12,64]{1,3,2,0:T(8,128)(2,1)} %copy.98) | copy-start | bytes 4538884
  418.2 4.1 copy-start
  462.0 8.4 %copy-start.1 = (f32[985,768]{1,0:T(8,128)S(1)}, f32[985,768]{1,0:T(8,128)}, u32[]{:S(2)}) copy-start(f32[985,768]{1,0:T(8,128)} %reshape.984) | copy-start | bytes 9077764
  462.0 8.4 %copy-start.16 = (f32[768]{0:T(1024)S(1)}, f32[768]{0:T(1024)}, u32[]{:S(2)}) copy-start(f32[768]{0:T(1024)} %copy-done.15) | copy-start | bytes 9220
  462.0 8.4 %copy-start.22 = (f32[768]{0:T(1024)S(1)}, f32[768]{0:T(1024)}, u32[]{:S(2)}) copy-start(f32[768]{0:T(1024)} %copy-done.21) | copy-start | bytes 9220
  470.4 8.5 %copy-start.12 = (f32[985,768]{1,0:T(8,128)S(1)}, f32[985,768]{1,0:T(8,128)}, u32[]{:S(2)}) copy-start(f32[985,768]{1,0:T(8,128)} %get-tuple-element.330) | copy-start | bytes 9077764
  480.9 4.4 copy-start.25
  485.3 8.8 %copy-start.11 = (bf16[985,768]{0,1:T(8,128)(2,1)S(1)}, bf16[985,768]{0,1:T(8,128)(2,1)}, u32[]{:S(2)}) copy-start(bf16[985,768]{0,1:T(8,128)(2,1)} %convert_element_type.321) | copy-start | bytes 4538884
  485.3 8.8 %copy-start.13 = (f32[985,768]{1,0:T(8,128)S(1)}, f32[985,768]{1,0:T(8,128)}, u32[]{:S(2)}) copy-start(f32[985,768]{1,0:T(8,128)} %get-tuple-element.330) | copy-start | bytes 9077764
  494.1 12.4 %slice-start = ((s8[6094848]{0:T(1024)(128)(4,1)}), s8[1900544]{0:T(1024)(128)(4,1)S(1)}, s32[]{:S(2)}) async-start(s8[6094848]{0:T(1024)(128)(4,1)} %bitcast.185), calls=%async_computation | async-start | bytes 3801088
  496.5 10.0 %copy-start.14 = (f32[985,768]{1,0:T(8,128)S(1)}, f32[985,768]{1,0:T(8,128)}, u32[]{:S(2)}) copy-start(f32[985,768]{1,0:T(8,128)} %reshape.996) | copy-start | bytes 9077764
  496.5 10.0 %slice-start.1 = ((s8[6094848]{0:T(1024)(128)(4,1)}), s8[4194304]{0:T(1024)(128)(4,1)S(1)}, s32[]{:S(2)}) async-start(s8[6094848]{0:T(1024)(128)(4,1)} %bitcast.185), calls=%async_computation.1 | async-start | bytes 8388608
  517.0 3.4 copy-start.9
  (6 other events, 11.2 us)

commit v2 on v1

--- a/solution.py
+++ b/solution.py
@@ -455,49 +455,408 @@
 
 
 norm_eps = 1e-06
-block_rows = 16
-
-
-def relative_index(row_ids, col_ids, grid_side):
-    table_rows = (2 * grid_side - 1) ** 2 + 3
-    rel_rows = row_ids - 1
-    rel_cols = col_ids - 1
-    down_diff = rel_rows // grid_side - rel_cols // grid_side + grid_side - 1
-    across_diff = rel_rows % grid_side - rel_cols % grid_side + grid_side - 1
-    inside = down_diff * (2 * grid_side - 1) + across_diff
-    first_row = row_ids == 0
-    first_col = col_ids == 0
-    position = jnp.where(first_row, table_rows - 3, jnp.where(first_col, table_rows - 2, inside))
-    position = jnp.where(first_row & first_col, table_rows - 1, position)
-    return position
-
-
-def position_onehot(block_id, seq_len, grid_side, table_rows):
-    row_ids = block_id * block_rows + jnp.arange(block_rows, dtype=jnp.int32)
-    col_ids = jnp.arange(seq_len, dtype=jnp.int32)
-    position = relative_index(row_ids[:, None], col_ids[None, :], grid_side)
-    position = jnp.where(row_ids[:, None] < seq_len, position, -1)
-    table_ids = jnp.arange(table_rows, dtype=jnp.int32)
-    onehot = (position[:, :, None] == table_ids[None, None, :]).astype(jnp.bfloat16)
-    return onehot.reshape(block_rows * seq_len, table_rows)
-
-
-def unpack(flat, shape):
-    entries = math.prod(shape)
-    return flat[:entries].reshape(shape)
-
-
-def pad_flat(values, length):
-    flat = values.reshape(-1)
-    return jnp.pad(flat, (0, length - flat.shape[0]))
-
-
-def normalize(values):
+
+
+RB = 200
+NEG = -1e30
+HEAD_QUAD = 4
+
+
+def params_of(limit=LIMIT, **kw):
+    return pltpu.CompilerParams(vmem_limit_bytes=limit, **kw)
+
+
+def row_norm(values):
     average = jnp.mean(values, axis=-1, keepdims=True)
     centred = values - average
     variance = jnp.mean(centred * centred, axis=-1, keepdims=True)
     inverse = lax.rsqrt(variance + norm_eps)
-    return (centred * inverse, inverse)
+    return centred * inverse, inverse
+
+
+def bias_build(tab_ref, bias_ref, rolled, spread, seq_len):
+    side = GRID
+    span = 2 * side - 1
+    wide = 384
+    tab = tab_ref[...]
+    for x in range(side):
+        rolled[pl.ds(x * 16, 16), :] = pltpu.roll(tab, (768 - x) % 768, 1).astype(jnp.bfloat16)
+    m = lax.broadcasted_iota(jnp.int32, (768, wide), 0)
+    n = lax.broadcasted_iota(jnp.int32, (768, wide), 1)
+    pick = (m == span * (span - 1 - n // side) + side - 1 - n % side) & (n < span * side)
+    onehot = jnp.where(pick, 1.0, 0.0).astype(jnp.bfloat16)
+    picked = jnp.dot(rolled[...], onehot, preferred_element_type=jnp.float32)
+    for n in range(wide // 128):
+        spread[n] = picked[:, n * 128 : n * 128 + 128]
+    lane = lax.broadcasted_iota(jnp.int32, (16, 768), 1)
+    base = span * span
+    row_first = jnp.sum(jnp.where(lane == base, tab, 0.0), axis=1, keepdims=True)
+    col_first = jnp.sum(jnp.where(lane == base + 1, tab, 0.0), axis=1, keepdims=True)
+    corner = jnp.sum(jnp.where(lane == base + 2, tab, 0.0), axis=1, keepdims=True)
+    cols = lax.broadcasted_iota(jnp.int32, (side, 256), 1)
+    top = lax.broadcasted_iota(jnp.int32, (1, 256), 1)
+    for h in range(HEADS):
+        rows = jnp.concatenate(
+            [spread[n, pl.ds(h, side, stride=16), :] for n in range(wide // 128)], axis=1
+        )
+        first = col_first[h : h + 1, :]
+        for y in range(side):
+            block = pltpu.roll(rows, (1 - (side - 1 - y) * side) % wide, 1)[:, :256]
+            block = jnp.where(cols == 0, first, jnp.where(cols < seq_len, block, NEG))
+            bias_ref[h, pl.ds(1 + side * y, side), :] = block[:, :RB]
+        line = jnp.where(top == 0, corner[h : h + 1, :], row_first[h : h + 1, :])
+        line = jnp.where(top < seq_len, line, NEG)
+        bias_ref[h, 0:1, :] = line[:, :RB]
+        bias_ref[h, pl.ds(seq_len, RB - seq_len), :] = jnp.where(
+            lax.broadcasted_iota(jnp.int32, (RB - seq_len, RB), 1) < seq_len, 0.0, NEG
+        )
+
+
+def attn_forward_kernel(
+    patches, mask, vecs, tab, qkv_w, out_w,
+    normed_o, qkv_o, probs_o, att_o, branch_o, middle_o,
+    x_s, bias_s, rolled, spread,
+):
+    images, seq_len, dim = patches.shape
+    bias_build(tab, bias_s, rolled, spread, seq_len)
+    token, gain, shift = vecs[0:1, :], vecs[1:2, :], vecs[2:3, :]
+
+    def load(i, _):
+        at = pl.multiple_of(i * RB, 8)
+        x_s[pl.ds(at + RB - 8, 8), :] = jnp.zeros((8, dim), jnp.float32)
+        rows = patches[i].astype(jnp.float32)
+        x_s[pl.ds(at, seq_len), :] = jnp.where(mask[i] > 0.5, token, rows)
+        normal, _ = row_norm(x_s[pl.ds(at, RB), :])
+        normed_o[pl.ds(at, RB), :] = (normal * gain + shift).astype(jnp.bfloat16)
+        return 0
+
+    lax.fori_loop(0, images, load, 0)
+    step = 256
+
+    def project(j, _):
+        col = pl.multiple_of(j * step, step)
+        value = jnp.dot(normed_o[...], qkv_w[:, pl.ds(col, step)], preferred_element_type=jnp.float32)
+        part = j // (dim // step)
+        inner = pl.multiple_of((j % (dim // step)) * step, step)
+        qb = vecs[3:4, pl.ds(inner, step)]
+        vb = vecs[4:5, pl.ds(inner, step)]
+        add = jnp.where(part == 0, qb, jnp.where(part == 2, vb, 0.0))
+        scale = jnp.where(part == 0, 0.125, 1.0)
+        qkv_o[:, pl.ds(col, step)] = ((value + add) * scale).astype(jnp.bfloat16)
+        return 0
+
+    lax.fori_loop(0, 3 * dim // step, project, 0)
+    lane = lax.broadcasted_iota(jnp.int32, (1, step), 1) // 64
+
+    def attend(n, _):
+        i, quad = n // 3, n % 3
+        at = pl.multiple_of(i * RB, 8)
+        col = pl.multiple_of(quad * step, step)
+        q = qkv_o[pl.ds(at, RB), pl.ds(col, step)]
+        k = qkv_o[pl.ds(at, RB), pl.ds(dim + col, step)]
+        v = qkv_o[pl.ds(at, RB), pl.ds(2 * dim + col, step)]
+        att = jnp.zeros((RB, step), jnp.float32)
+        for j in range(HEAD_QUAD):
+            mine = lane == j
+            qj = jnp.where(mine, q, jnp.zeros_like(q))
+            s = lax.dot_general(qj, k, (((1,), (1,)), ((), ())), preferred_element_type=jnp.float32)
+            s = s + bias_s[quad * HEAD_QUAD + j]
+            e = jnp.exp(s - jnp.max(s, axis=1, keepdims=True))
+            p = (e / jnp.sum(e, axis=1, keepdims=True)).astype(jnp.bfloat16)
+            probs_o[i * HEADS + quad * HEAD_QUAD + j] = p
+            o = jnp.dot(p, v, preferred_element_type=jnp.float32)
+            att = jnp.where(mine, o, att)
+        att_o[pl.ds(at, RB), pl.ds(col, step)] = att.astype(jnp.bfloat16)
+        return 0
+
+    lax.fori_loop(0, images * 3, attend, 0)
+
+    def leave(j, _):
+        col = pl.multiple_of(j * step, step)
+        value = jnp.dot(att_o[...], out_w[:, pl.ds(col, step)], preferred_element_type=jnp.float32)
+        value = value + vecs[5:6, pl.ds(col, step)]
+        branch_o[:, pl.ds(col, step)] = value
+        middle_o[:, pl.ds(col, step)] = x_s[:, pl.ds(col, step)] + vecs[6:7, pl.ds(col, step)] * value
+        return 0
+
+    lax.fori_loop(0, dim // step, leave, 0)
+
+
+def attn_forward(patches, mask, vecs, tab, qkv_w, out_w):
+    images, seq_len, dim = patches.shape
+    rows = images * RB
+    f32, bf16 = jnp.float32, jnp.bfloat16
+    S = jax.ShapeDtypeStruct
+    return pl.pallas_call(
+        attn_forward_kernel,
+        out_shape=[
+            S((rows, dim), bf16), S((rows, 3 * dim), bf16), S((images * HEADS, RB, RB), bf16),
+            S((rows, dim), bf16), S((rows, dim), f32), S((rows, dim), f32),
+        ],
+        in_specs=[VMEM] * 6,
+        out_specs=[VMEM] * 6,
+        scratch_shapes=[
+            pltpu.VMEM((rows, dim), f32), pltpu.VMEM((HEADS, RB, RB), f32),
+            pltpu.VMEM((GRID * 16, 768), bf16), pltpu.VMEM((3, GRID * 16, 128), f32),
+        ],
+        compiler_params=params_of(),
+        name="attn_fwd",
+    )(patches, mask, vecs, tab, qkv_w, out_w)
+
+
+def contract(left, right, dim_left, dim_right):
+    return lax.dot_general(
+        left, right, (((dim_left,), (dim_right,)), ((), ())), preferred_element_type=jnp.float32
+    )
+
+
+def mlp_kernel(
+    middle, cotangent, mask, vecs, up_b, up_w, down_w,
+    layer_o, grad_middle_o, up_grad_o, down_grad_o, vec_o, up_b_o,
+    go_s, gd_s, xn_s, down_s, dx_s,
+):
+    images, seq_len, dim = cotangent.shape
+    rows = images * RB
+    hidden_dim = up_w.shape[1]
+    post_g, post_s = vecs[7:8, :], vecs[8:9, :]
+    down_b, mlp_g = vecs[9:10, :], vecs[10:11, :]
+    step = 256
+    vec_o[...] = jnp.zeros_like(vec_o)
+    down_s[...] = jnp.zeros_like(down_s)
+    dx_s[...] = jnp.zeros_like(dx_s)
+
+    def load(i, _):
+        at = pl.multiple_of(i * RB, 8)
+        go_s[pl.ds(at + RB - 8, 8), :] = jnp.zeros((8, dim), jnp.float32)
+        grad = cotangent[i].astype(jnp.float32)
+        go_s[pl.ds(at, seq_len), :] = jnp.where(mask[i] > 0.5, grad, 0.0)
+        grad = go_s[pl.ds(at, RB), :] * mlp_g
+        vec_o[9:10, :] += jnp.sum(grad, axis=0, keepdims=True)
+        gd_s[pl.ds(at, RB), :] = grad.astype(jnp.bfloat16)
+        normal, _ = row_norm(middle[pl.ds(at, RB), :])
+        xn_s[pl.ds(at, RB), :] = (normal * post_g + post_s).astype(jnp.bfloat16)
+        return 0
+
+    lax.fori_loop(0, images, load, 0)
+
+    def chunk(j, _):
+        col = pl.multiple_of(j * step, step)
+        up_c = up_w[:, pl.ds(col, step)]
+        down_c = down_w[pl.ds(col, step), :]
+        xn, gd = xn_s[...], gd_s[...]
+        up = jnp.dot(xn, up_c, preferred_element_type=jnp.float32) + up_b[0:1, pl.ds(col, step)]
+        cdf = 0.5 * (1.0 + lax.erf(up * 0.7071067811865476))
+        hidden = (up * cdf).astype(jnp.bfloat16)
+        slope = cdf + up * jnp.exp(-0.5 * up * up) * 0.3989422804014327
+        grad = contract(gd, down_c, 1, 1) * slope
+        up_b_o[0:1, pl.ds(col, step)] = jnp.sum(grad, axis=0, keepdims=True)
+        gu = grad.astype(jnp.bfloat16)
+        down_s[...] += jnp.dot(hidden, down_c, preferred_element_type=jnp.float32)
+        dx_s[...] += contract(gu, up_c, 1, 1)
+        down_grad_o[pl.ds(col, step), :] = contract(hidden, gd, 0, 0).astype(jnp.bfloat16)
+        up_grad_o[:, pl.ds(col, step)] = contract(xn, gu, 0, 0).astype(jnp.bfloat16)
+        return 0
+
+    lax.fori_loop(0, hidden_dim // step, chunk, 0)
+
+    def leave(i, _):
+        at = pl.multiple_of(i * RB, 8)
+        go = go_s[pl.ds(at, RB), :]
+        mid = middle[pl.ds(at, RB), :]
+        down_rows = down_s[pl.ds(at, RB), :] + down_b
+        layer_o[i] = (mid + mlp_g * down_rows)[:seq_len].astype(jnp.bfloat16)
+        vec_o[10:11, :] += jnp.sum(go * down_rows, axis=0, keepdims=True)
+        grad = dx_s[pl.ds(at, RB), :]
+        normal, inverse = row_norm(mid)
+        vec_o[7:8, :] += jnp.sum(grad * normal, axis=0, keepdims=True)
+        vec_o[8:9, :] += jnp.sum(grad, axis=0, keepdims=True)
+        grad_middle_o[pl.ds(at, RB), :] = go + norm_back(grad, normal, inverse, post_g)
+        return 0
+
+    lax.fori_loop(0, images, leave, 0)
+
+
+def mlp(middle, cotangent, mask, vecs, up_b, up_w, down_w):
+    images, seq_len, dim = cotangent.shape
+    rows = images * RB
+    f32, bf16 = jnp.float32, jnp.bfloat16
+    S = jax.ShapeDtypeStruct
+    return pl.pallas_call(
+        mlp_kernel,
+        out_shape=[
+            S(cotangent.shape, bf16), S((rows, dim), f32), S(up_w.shape, bf16), S(down_w.shape, bf16),
+            S((16, dim), f32), S(up_b.shape, f32),
+        ],
+        in_specs=[VMEM] * 7,
+        out_specs=[VMEM] * 6,
+        scratch_shapes=[
+            pltpu.VMEM((rows, dim), f32), pltpu.VMEM((rows, dim), bf16), pltpu.VMEM((rows, dim), bf16),
+            pltpu.VMEM((rows, dim), f32), pltpu.VMEM((rows, dim), f32),
+        ],
+        compiler_params=params_of(),
+        name="mlp",
+    )(middle, cotangent, mask, vecs, up_b, up_w, down_w)
+
+
+def table_build(db, out_ref, rows_s, seq_len):
+    side = GRID
+    span = 2 * side - 1
+    wide = 384
+    rows_s[...] = jnp.zeros_like(rows_s)
+    lane = lax.broadcasted_iota(jnp.int32, (1, RB), 1)
+    out_lane = lax.broadcasted_iota(jnp.int32, (1, 768), 1)
+    base = span * span
+    for h in range(HEADS):
+        total = jnp.zeros((side, wide), jnp.float32)
+        for y in range(side):
+            block = db[h, pl.ds(1 + side * y, side), :]
+            block = jnp.where((lane > 0) & (lane < seq_len), block, 0.0)
+            block = jnp.concatenate([block, jnp.zeros((side, wide - RB), jnp.float32)], axis=1)
+            total += pltpu.roll(block, ((side - 1 - y) * side - 1) % wide, 1)
+        for n in range(wide // 128):
+            rows_s[n, pl.ds(h, side, stride=16), :] = total[:, n * 128 : n * 128 + 128]
+    m = lax.broadcasted_iota(jnp.int32, (wide, 768), 1)
+    n = lax.broadcasted_iota(jnp.int32, (wide, 768), 0)
+    pick = (m == span * (span - 1 - n // side) + side - 1 - n % side) & (n < span * side)
+    onehot = jnp.where(pick, 1.0, 0.0).astype(jnp.bfloat16)
+    total = jnp.zeros((16, 768), jnp.float32)
+    for x in range(side):
+        rows = jnp.concatenate([rows_s[k, pl.ds(x * 16, 16), :] for k in range(wide // 128)], axis=1)
+        upper = rows.astype(jnp.bfloat16)
+        lower = (rows - upper.astype(jnp.float32)).astype(jnp.bfloat16)
+        part = jnp.dot(upper, onehot, preferred_element_type=jnp.float32)
+        part += jnp.dot(lower, onehot, preferred_element_type=jnp.float32)
+        total += pltpu.roll(part, x, 1)
+    out_ref[...] = total
+    for h in range(HEADS):
+        top = db[h, 0:1, :]
+        corner = jnp.sum(jnp.where(lane == 0, top, 0.0), axis=1, keepdims=True)
+        first_row = jnp.sum(jnp.where(lane > 0, top, 0.0), axis=1, keepdims=True)
+        col = jnp.sum(db[h], axis=0, keepdims=True)
+        first_col = jnp.sum(jnp.where(lane == 0, col, 0.0), axis=1, keepdims=True) - corner
+        line = out_ref[h : h + 1, :]
+        line = jnp.where(out_lane == base, first_row, line)
+        line = jnp.where(out_lane == base + 1, first_col, line)
+        out_ref[h : h + 1, :] = jnp.where(out_lane == base + 2, corner, line)
+
+
+def attn_backward_kernel(
+    grad_middle, branch, att, qkv, probs, normed, patches, mask, vecs, qkv_w, out_w,
+    patch_o, qkv_grad_o, out_grad_o, vec_o, tab_o,
+    gb_s, ga_s, gproj_s, gnp_s, db_s, rows_s,
+):
+    images, seq_len, dim = patches.shape
+    token, gain, scale = vecs[0:1, :], vecs[1:2, :], vecs[6:7, :]
+    step = 256
+    vec_o[...] = jnp.zeros_like(vec_o)
+    db_s[...] = jnp.zeros_like(db_s)
+
+    def enter(i, _):
+        at = pl.multiple_of(i * RB, 8)
+        grad = grad_middle[pl.ds(at, RB), :]
+        vec_o[6:7, :] += jnp.sum(grad * branch[pl.ds(at, RB), :], axis=0, keepdims=True)
+        grad = grad * scale
+        vec_o[5:6, :] += jnp.sum(grad, axis=0, keepdims=True)
+        gb_s[pl.ds(at, RB), :] = grad.astype(jnp.bfloat16)
+        return 0
+
+    lax.fori_loop(0, images, enter, 0)
+
+    def out_part(j, _):
+        col = pl.multiple_of(j * step, step)
+        ga_s[:, pl.ds(col, step)] = contract(gb_s[...], out_w[pl.ds(col, step), :], 1, 1).astype(jnp.bfloat16)
+        out_grad_o[:, pl.ds(col, step)] = contract(att[...], gb_s[:, pl.ds(col, step)], 0, 0).astype(jnp.bfloat16)
+        return 0
+
+    lax.fori_loop(0, dim // step, out_part, 0)
+    lane = lax.broadcasted_iota(jnp.int32, (1, step), 1) // 64
+
+    def attend(n, _):
+        quad, i = n // images, n % images
+        at = pl.multiple_of(i * RB, 8)
+        col = pl.multiple_of(quad * step, step)
+        q = qkv[pl.ds(at, RB), pl.ds(col, step)]
+        k = qkv[pl.ds(at, RB), pl.ds(dim + col, step)]
+        v = qkv[pl.ds(at, RB), pl.ds(2 * dim + col, step)]
+        ga = ga_s[pl.ds(at, RB), pl.ds(col, step)]
+        zero = jnp.zeros((RB, step), jnp.float32)
+        gq, gk, gv = zero, zero, zero
+        for j in range(HEAD_QUAD):
+            mine = lane == j
+            h = quad * HEAD_QUAD + j
+            p = probs[i * HEADS + h]
+            gp = contract(jnp.where(mine, ga, jnp.zeros_like(ga)), v, 1, 1)
+            gv = jnp.where(mine, contract(p, ga, 0, 0), gv)
+            pf = p.astype(jnp.float32)
+            gs = pf * (gp - jnp.sum(pf * gp, axis=1, keepdims=True))
+            db_s[h] += gs
+            low = gs.astype(jnp.bfloat16)
+            gq = jnp.where(mine, jnp.dot(low, k, preferred_element_type=jnp.float32), gq)
+            gk = jnp.where(mine, contract(low, q, 0, 0), gk)
+        gq = gq * 0.125
+        vec_o[3:4, pl.ds(col, step)] += jnp.sum(gq, axis=0, keepdims=True)
+        vec_o[4:5, pl.ds(col, step)] += jnp.sum(gv, axis=0, keepdims=True)
+        gproj_s[pl.ds(at, RB), pl.ds(col, step)] = gq.astype(jnp.bfloat16)
+        gproj_s[pl.ds(at, RB), pl.ds(dim + col, step)] = gk.astype(jnp.bfloat16)
+        gproj_s[pl.ds(at, RB), pl.ds(2 * dim + col, step)] = gv.astype(jnp.bfloat16)
+        return 0
+
+    lax.fori_loop(0, images * 3, attend, 0)
+
+    def qkv_part(j, _):
+        col = pl.multiple_of(j * step, step)
+        qkv_grad_o[:, pl.ds(col, step)] = contract(normed[...], gproj_s[:, pl.ds(col, step)], 0, 0).astype(
+            jnp.bfloat16
+        )
+        return 0
+
+    lax.fori_loop(0, 3 * dim // step, qkv_part, 0)
+
+    def back(j, _):
+        col = pl.multiple_of(j * step, step)
+        gnp_s[:, pl.ds(col, step)] = contract(gproj_s[...], qkv_w[pl.ds(col, step), :], 1, 1)
+        return 0
+
+    lax.fori_loop(0, dim // step, back, 0)
+
+    def leave(i, _):
+        at = pl.multiple_of(i * RB, 8)
+        here = mask[i] > 0.5
+        rows = jnp.where(here, token, patches[i].astype(jnp.float32))
+        normal, inverse = row_norm(rows)
+        grad = gnp_s[pl.ds(at, RB), :][:seq_len]
+        vec_o[1:2, :] += jnp.sum(grad * normal, axis=0, keepdims=True)
+        vec_o[2:3, :] += jnp.sum(grad, axis=0, keepdims=True)
+        grad = grad_middle[pl.ds(at, RB), :][:seq_len] + norm_back(grad, normal, inverse, gain)
+        vec_o[0:1, :] += jnp.sum(jnp.where(here, grad, 0.0), axis=0, keepdims=True)
+        patch_o[i] = jnp.where(here, 0.0, grad).astype(jnp.bfloat16)
+        return 0
+
+    lax.fori_loop(0, images, leave, 0)
+    table_build(db_s, tab_o, rows_s, seq_len)
+
+
+def attn_backward(grad_middle, branch, att, qkv, probs, normed, patches, mask, vecs, qkv_w, out_w):
+    images, seq_len, dim = patches.shape
+    rows = images * RB
+    f32, bf16 = jnp.float32, jnp.bfloat16
+    S = jax.ShapeDtypeStruct
+    return pl.pallas_call(
+        attn_backward_kernel,
+        out_shape=[
+            S(patches.shape, bf16), S(qkv_w.shape, bf16), S(out_w.shape, bf16), S((16, dim), f32),
+            S((16, 768), f32),
+        ],
+        in_specs=[VMEM] * 11,
+        out_specs=[VMEM] * 5,
+        scratch_shapes=[
+            pltpu.VMEM((rows, dim), bf16), pltpu.VMEM((rows, dim), bf16), pltpu.VMEM((rows, 3 * dim), bf16),
+            pltpu.VMEM((rows, dim), f32), pltpu.VMEM((HEADS, RB, RB), f32),
+            pltpu.VMEM((3, GRID * 16, 128), f32),
+        ],
+        compiler_params=params_of(),
+        name="attn_bwd",
+    )(grad_middle, branch, att, qkv, probs, normed, patches, mask, vecs, qkv_w, out_w)
 
 
 def norm_back(grad_normed, normal, inverse, gain):
@@ -507,219 +866,54 @@
     return inverse * (scaled - first_mean - normal * second_mean)
 
 
-def gelu_slope(values):
-    return (
-        0.5 * (1.0 + lax.erf(values * 0.7071067811865476))
-        + values * jnp.exp(-0.5 * values * values) * 0.3989422804014327
-    )
-
-
 def per_device(
-    patches,
-    patch_mask,
-    cotangent,
-    mask_token,
-    pre_gain,
-    pre_shift,
-    qkv_weight,
-    query_bias,
-    value_bias,
-    rel_table,
-    out_weight,
-    out_bias,
-    attn_scale,
-    post_gain,
-    post_shift,
-    up_weight,
-    up_bias,
-    down_weight,
-    down_bias,
-    mlp_scale,
+    patches, patch_mask, cotangent, mask_token, pre_gain, pre_shift, qkv_weight, query_bias, value_bias,
+    rel_table, out_weight, out_bias, attn_scale, post_gain, post_shift, up_weight, up_bias, down_weight,
+    down_bias, mlp_scale,
 ):
-    images, seq_len, model_dim = patches.shape
-    heads = HEADS
-    head_dim = model_dim // heads
-    hidden_dim = FF
-    grid_side = GRID
+    images, seq_len, dim = patches.shape
     table_rows = (2 * GRID - 1) ** 2 + 3
-    block_count = -(-seq_len // block_rows)
-    padded_rows = block_count * block_rows
-    four_dims = (images, seq_len, heads, head_dim)
-    total_devices = lax.axis_size(("dp", "fsdp"))
+    devices = lax.axis_size(("dp", "fsdp"))
     sizes = mesh_sizes(lax.axis_size("dp"), lax.axis_size("fsdp"))
     vec_shards = (
         mask_token, pre_gain, pre_shift, query_bias, value_bias, out_bias, attn_scale,
         post_gain, post_shift, down_bias, mlp_scale,
     )
     small = pack_small(vec_shards, up_bias, rel_table)
-    widths = (3 * model_dim, model_dim, hidden_dim, model_dim)
+    widths = (3 * dim, dim, FF, dim)
     mats = (qkv_weight, out_weight, up_weight, down_weight)
     blocks = [m.reshape(block_shape(m.shape[0], w)) for m, w in zip(mats, widths)]
     small_full, *mats_full = gather_call(sizes, [small] + blocks, 0)
     qkv_w, out_w, up_w, down_w = [m.reshape(-1, w) for m, w in zip(mats_full, widths)]
-    rows_full = small_full.reshape(total_devices, TILE, 128)
+    rows_full = small_full.reshape(devices, TILE, 128).astype(jnp.float32)
     per_vec = mask_token.shape[0]
-    vectors = [rows_full[:, i, :per_vec].reshape(-1).astype(jnp.float32) for i in range(11)]
-    (
-        token_fill, pre_g, pre_s, query_b, value_b, out_b, attn_g, post_g, post_s, down_b, mlp_g,
-    ) = vectors
-    up_b = rows_full[:, 11, : up_bias.shape[0]].reshape(-1).astype(jnp.float32)
-    table = rows_full[:, 12:].reshape(total_devices, -1)[:, : rel_table.shape[0]].reshape(-1)
-    table = table[: table_rows * heads].reshape(table_rows, heads)
-    masked = patch_mask.reshape(-1, 1) == 1
-    token_rows = patches.reshape(-1, model_dim).astype(jnp.float32)
-    initial = jnp.where(masked, token_fill[None, :], token_rows)
-    normal_pre, inverse_pre = normalize(initial)
-    normed_pre = (normal_pre * pre_g + pre_s).astype(jnp.bfloat16)
-    projected = jnp.dot(normed_pre, qkv_w, preferred_element_type=jnp.float32)
-    queries = ((projected[:, :model_dim] + query_b) * 0.125).astype(jnp.bfloat16).reshape(four_dims)
-    keys_all = projected[:, model_dim : 2 * model_dim].astype(jnp.bfloat16).reshape(four_dims)
-    values_all = (projected[:, 2 * model_dim :] + value_b).astype(jnp.bfloat16).reshape(four_dims)
-
-    def bias_rows(block_id):
-        onehot = position_onehot(block_id, seq_len, grid_side, table_rows)
-        return jnp.einsum("rh,ar->ha", table, onehot, preferred_element_type=jnp.float32)
-
-    bias_pieces = lax.map(bias_rows, jnp.arange(block_count, dtype=jnp.int32))
-    bias_pieces = bias_pieces.reshape(block_count, heads, block_rows, seq_len)
-    pos_bias = jnp.transpose(bias_pieces, (1, 0, 2, 3)).reshape(heads, padded_rows, seq_len)[
-        :, :seq_len
-    ]
-    scores = (
-        jnp.einsum("ishd,ithd->ihst", queries, keys_all, preferred_element_type=jnp.float32)
-        + pos_bias[None]
+    vecs = jnp.transpose(rows_full[:, :11, :per_vec], (1, 0, 2)).reshape(11, dim)
+    vecs = jnp.pad(vecs, ((0, 5), (0, 0)))
+    up_b = rows_full[:, 11, : up_bias.shape[0]].reshape(1, FF)
+    table = rows_full[:, 12:].reshape(devices, -1)[:, : rel_table.shape[0]].reshape(-1)
+    table = table[: table_rows * HEADS].reshape(table_rows, HEADS).T
+    table = jnp.pad(table, ((0, 16 - HEADS), (0, 768 - table_rows)))
+    mask = patch_mask.astype(jnp.float32)[:, :, None]
+    normed, qkv, probs, att, branch, middle = attn_forward(patches, mask, vecs, table, qkv_w, out_w)
+    layer_out, grad_middle, up_grad, down_grad, vec_mlp, up_b_grad = mlp(
+        middle, cotangent, mask, vecs, up_b, up_w, down_w
     )
-    peak = jnp.max(scores, axis=-1, keepdims=True)
-    shifted = jnp.exp(scores - peak)
-    totals = jnp.sum(shifted, axis=-1, keepdims=True)
-    probs = shifted / totals
-    log_total = peak + jnp.log(totals)
-    attended = jnp.einsum(
-        "ihst,ithd->ishd",
-        probs.astype(jnp.bfloat16),
-        values_all,
-        preferred_element_type=jnp.float32,
+    patch_grad, qkv_grad, out_grad, vec_attn, table_grad = attn_backward(
+        grad_middle, branch, att, qkv, probs, normed, patches, mask, vecs, qkv_w, out_w
     )
-    attended = attended.reshape(-1, model_dim).astype(jnp.bfloat16)
-    branch = jnp.dot(attended, out_w, preferred_element_type=jnp.float32) + out_b
-    middle = initial + attn_g * branch
-    normal_post, inverse_post = normalize(middle)
-    normed_post = (normal_post * post_g + post_s).astype(jnp.bfloat16)
-    up_rows = jnp.dot(normed_post, up_w, preferred_element_type=jnp.float32) + up_b
-    hidden = jax.nn.gelu(up_rows, approximate=False).astype(jnp.bfloat16)
-    down_rows = jnp.dot(hidden, down_w, preferred_element_type=jnp.float32) + down_b
-    result = middle + mlp_g * down_rows
-    layer_out = result.astype(jnp.bfloat16).reshape(patches.shape)
-    grad_out = cotangent.reshape(-1, model_dim).astype(jnp.float32) * masked.astype(jnp.float32)
-    mlp_scale_grad = jnp.sum(grad_out * down_rows, axis=0)
-    grad_down_rows = mlp_g * grad_out
-    down_bias_grad = jnp.sum(grad_down_rows, axis=0)
-    grad_down = grad_down_rows.astype(jnp.bfloat16)
-    down_weight_grad = jnp.einsum(
-        "ra,rb->ab", hidden, grad_down, preferred_element_type=jnp.float32
+    vec_grad = jnp.concatenate([vec_attn[:7], vec_mlp[7:11]]).reshape(11, devices, per_vec)
+    vec_grad = jnp.pad(jnp.transpose(vec_grad, (1, 0, 2)), ((0, 0), (0, 0), (0, 128 - per_vec)))
+    up_b_grad = up_b_grad.reshape(devices, 1, -1)
+    up_b_grad = jnp.pad(up_b_grad, ((0, 0), (0, 0), (0, 128 - up_b_grad.shape[2])))
+    table_flat = table_grad[:HEADS, :table_rows].T.reshape(-1)
+    table_flat = jnp.pad(table_flat, (0, devices * rel_table.shape[0] - table_flat.shape[0]))
+    table_flat = table_flat.reshape(devices, -1)
+    table_flat = jnp.pad(table_flat, ((0, 0), (0, (TILE - 12) * 128 - table_flat.shape[1])))
+    small_grad = jnp.concatenate(
+        [vec_grad, up_b_grad, table_flat.reshape(devices, TILE - 12, 128)], axis=1
     )
-    grad_hidden = jnp.einsum("rb,ab->ra", grad_down, down_w, preferred_element_type=jnp.float32)
-    grad_up_rows = grad_hidden * gelu_slope(up_rows)
-    up_bias_grad = jnp.sum(grad_up_rows, axis=0)
-    grad_up = grad_up_rows.astype(jnp.bfloat16)
-    up_weight_grad = jnp.einsum(
-        "ra,rb->ab", normed_post, grad_up, preferred_element_type=jnp.float32
-    )
-    grad_normed_post = jnp.einsum("rb,ab->ra", grad_up, up_w, preferred_element_type=jnp.float32)
-    post_gain_grad = jnp.sum(grad_normed_post * normal_post, axis=0)
-    post_shift_grad = jnp.sum(grad_normed_post, axis=0)
-    grad_middle = grad_out + norm_back(grad_normed_post, normal_post, inverse_post, post_g)
-    attn_scale_grad = jnp.sum(grad_middle * branch, axis=0)
-    grad_branch_rows = attn_g * grad_middle
-    out_bias_grad = jnp.sum(grad_branch_rows, axis=0)
-    grad_branch = grad_branch_rows.astype(jnp.bfloat16)
-    out_weight_grad = jnp.einsum(
-        "ra,rb->ab", attended, grad_branch, preferred_element_type=jnp.float32
-    )
-    grad_attended = jnp.einsum("rb,ab->ra", grad_branch, out_w, preferred_element_type=jnp.float32)
-    grad_attended = grad_attended.astype(jnp.bfloat16).reshape(four_dims)
-    scores_again = (
-        jnp.einsum("ishd,ithd->ihst", queries, keys_all, preferred_element_type=jnp.float32)
-        + pos_bias[None]
-    )
-    probs_again = jnp.exp(scores_again - log_total)
-    grad_probs = jnp.einsum(
-        "ishd,ithd->ihst", grad_attended, values_all, preferred_element_type=jnp.float32
-    )
-    grad_values = jnp.einsum(
-        "ihst,ishd->ithd",
-        probs_again.astype(jnp.bfloat16),
-        grad_attended,
-        preferred_element_type=jnp.float32,
-    )
-    inner_sum = jnp.sum(probs_again * grad_probs, axis=-1, keepdims=True)
-    grad_scores = probs_again * (grad_probs - inner_sum)
-    bias_grad = jnp.sum(grad_scores, axis=0)
-    grad_scores_low = grad_scores.astype(jnp.bfloat16)
-    grad_queries = (
-        jnp.einsum("ihst,ithd->ishd", grad_scores_low, keys_all, preferred_element_type=jnp.float32)
-        * 0.125
-    )
-    grad_keys = jnp.einsum(
-        "ihst,ishd->ithd", grad_scores_low, queries, preferred_element_type=jnp.float32
-    )
-    grad_queries = grad_queries.reshape(-1, model_dim)
-    grad_keys = grad_keys.reshape(-1, model_dim)
-    grad_values = grad_values.reshape(-1, model_dim)
-    query_bias_grad = jnp.sum(grad_queries, axis=0)
-    value_bias_grad = jnp.sum(grad_values, axis=0)
-    grad_projected = jnp.concatenate([grad_queries, grad_keys, grad_values], axis=1).astype(
-        jnp.bfloat16
-    )
-    qkv_weight_grad = jnp.einsum(
-        "ra,rb->ab", normed_pre, grad_projected, preferred_element_type=jnp.float32
-    )
-    grad_normed_pre = jnp.einsum(
-        "rb,ab->ra", grad_projected, qkv_w, preferred_element_type=jnp.float32
-    )
-    pre_gain_grad = jnp.sum(grad_normed_pre * normal_pre, axis=0)
-    pre_shift_grad = jnp.sum(grad_normed_pre, axis=0)
-    grad_initial = grad_middle + norm_back(grad_normed_pre, normal_pre, inverse_pre, pre_g)
-    mask_token_grad = jnp.sum(jnp.where(masked, grad_initial, 0.0), axis=0)
-    patch_grad = jnp.where(masked, 0.0, grad_initial).astype(jnp.bfloat16).reshape(patches.shape)
-    bias_grid = jnp.pad(bias_grad, ((0, 0), (0, padded_rows - seq_len), (0, 0)))
-    bias_grid = bias_grid.reshape(heads, block_count, block_rows * seq_len)
-    bias_grid = jnp.transpose(bias_grid, (1, 0, 2))
-
-    def add_block(running, inputs):
-        block_id, piece = inputs
-        onehot = position_onehot(block_id, seq_len, grid_side, table_rows)
-        upper = piece.astype(jnp.bfloat16)
-        lower = (piece - upper.astype(jnp.float32)).astype(jnp.bfloat16)
-        running = running + jnp.dot(upper, onehot, preferred_element_type=jnp.float32)
-        running = running + jnp.dot(lower, onehot, preferred_element_type=jnp.float32)
-        return (running, None)
-
-    table_grad_t, _ = lax.scan(
-        add_block,
-        jnp.zeros((heads, table_rows), jnp.float32),
-        (jnp.arange(block_count, dtype=jnp.int32), bias_grid),
-    )
-    table_grad = jnp.transpose(table_grad_t)
-    vec_grads = (
-        mask_token_grad, pre_gain_grad, pre_shift_grad, query_bias_grad, value_bias_grad,
-        out_bias_grad, attn_scale_grad, post_gain_grad, post_shift_grad, down_bias_grad,
-        mlp_scale_grad,
-    )
-    table_flat = pad_flat(table_grad, rel_table.shape[0] * total_devices)
-
-    def lanes(value, count):
-        value = value.reshape(total_devices, -1)
-        return jnp.pad(value, ((0, 0), (0, count - value.shape[1])))
-
-    small_grad = jnp.concatenate(
-        [lanes(v, 128) for v in vec_grads]
-        + [lanes(up_bias_grad, 128), lanes(table_flat, (TILE - 12) * 128)],
-        axis=1,
-    ).reshape(total_devices, TILE, 128)
-    mat_grads = (qkv_weight_grad, out_weight_grad, up_weight_grad, down_weight_grad)
     partials = [
-        g.astype(jnp.bfloat16).reshape(total_devices, *b.shape) for g, b in zip(mat_grads, blocks)
+        g.reshape(devices, *b.shape) for g, b in zip((qkv_grad, out_grad, up_grad, down_grad), blocks)
     ]
     *mat_own, small_own = reduce_call(sizes, partials + [small_grad], 1)
     qkv_o, out_o, up_o, down_o = [m.reshape(-1) for m in mat_own]
@@ -738,49 +932,10 @@
 
 
 def solution(mesh):
-    in_specs = (
-        P(("dp", "fsdp"), None, None),
-        P(("dp", "fsdp"), None),
-        P(("dp", "fsdp"), None, None),
-        P(("dp", "fsdp")),
-        P(("dp", "fsdp")),
-        P(("dp", "fsdp")),
-        P(("dp", "fsdp")),
-        P(("dp", "fsdp")),
-        P(("dp", "fsdp")),
-        P(("dp", "fsdp")),
-        P(("dp", "fsdp")),
-        P(("dp", "fsdp")),
-        P(("dp", "fsdp")),
-        P(("dp", "fsdp")),
-        P(("dp", "fsdp")),
-        P(("dp", "fsdp")),
-        P(("dp", "fsdp")),
-        P(("dp", "fsdp")),
-        P(("dp", "fsdp")),
-        P(("dp", "fsdp")),
-    )
-    out_specs = (
-        P(("dp", "fsdp"), None, None),
-        P(("dp", "fsdp"), None, None),
-        P(("dp", "fsdp")),
-        P(("dp", "fsdp")),
-        P(("dp", "fsdp")),
-        P(("dp", "fsdp")),
-        P(("dp", "fsdp")),
-        P(("dp", "fsdp")),
-        P(("dp", "fsdp")),
-        P(("dp", "fsdp")),
-        P(("dp", "fsdp")),
-        P(("dp", "fsdp")),
-        P(("dp", "fsdp")),
-        P(("dp", "fsdp")),
-        P(("dp", "fsdp")),
-        P(("dp", "fsdp")),
-        P(("dp", "fsdp")),
-        P(("dp", "fsdp")),
-        P(("dp", "fsdp")),
-    )
+    split = ("dp", "fsdp")
+    rows = P(split, None, None)
+    in_specs = (rows, P(split, None), rows) + (P(split),) * 17
+    out_specs = (rows, rows) + (P(split),) * 17
     return jax.shard_map(
         per_device, mesh=mesh, in_specs=in_specs, out_specs=out_specs, check_vma=False
     )

time: 754 us -> 374 us (0.50); the launches traced: 743 us -> 374 us
  matrix products: 258 us -> 0 us
  local copies, waits for them, and re-layouts: 226 us -> 36.3 us
  Pallas kernels: 198 us -> 334 us
  other arithmetic: 41.6 us -> 2.37 us
  loops' own time: 19.1 us -> 0 us
    dot_general x57 -> x0, matrix products: 258 us -> none  [the longest x1 35.8 us: per_device(): jnp.dot(normed_post, up_w, preferred_element_type=jnp.float32) + up_b]
    pallas_call x0 -> x3, Pallas kernels: none -> 137 us  [the longest x1 50.9 us: attn_backward(): pl.pallas_call(attn_backward_kernel, out_shape=[S(patches.shape, bf16), S...]
    reshape x32 -> x8, local copies, waits for them, and re-layouts: 79.9 us -> 1.44 us  [the longest x2 0.56 us: per_device(): table = table[:table_rows * HEADS].reshape(table_rows, HEADS).T]
    dynamic_slice x39 -> x0, local copies, waits for them, and re-layouts: 33.4 us -> none  [the longest x13 18.2 us: per_device(): lax.scan(add_block, jnp.zeros((heads, table_rows), jnp.float32), (jnp.ara...]
    reduce_sum x9 -> x0, other arithmetic: 31.1 us -> none  [the longest x1 11.6 us: per_device(): bias_grad = jnp.sum(grad_scores, axis=0)]
    convert_element_type x18 -> x0, local copies, waits for them, and re-layouts: 20 us -> none  [the longest x2 8.81 us: per_device(): attended = attended.reshape(-1, model_dim).astype(jnp.bfloat16)]
    another operation x2 -> x0, loops' own time: 19.1 us -> none  [the longest x1 9.72 us: per_device(): lax.scan(add_block, jnp.zeros((heads, table_rows), jnp.float32), (jnp.ara...]
    sub x208 -> x0, local copies, waits for them, and re-layouts: 15.1 us -> none  [the longest x104 7.57 us: relative_index(): across_diff = rel_rows % grid_side - rel_cols % grid_side + grid_side - 1]
where the time goes in v2:
time: 374 us
  Pallas kernels  334 us (89%)
  local copies, waits for them, and re-layouts  36.3 us (10%)
    pallas_call x1, Pallas kernels, reduce_call(): pl.pallas_call(functools.partial(reduce_kernel, sizes, n), out_shape=shap...  104 us
    pallas_call x1, Pallas kernels, gather_call(): pl.pallas_call(functools.partial(gather_kernel, sizes, n), out_shape=shap...  93.2 us
    pallas_call x1, Pallas kernels, attn_backward(): pl.pallas_call(attn_backward_kernel, out_shape=[S(patches.shape, bf16), S...  50.9 us
    pallas_call x1, Pallas kernels, mlp(): pl.pallas_call(mlp_kernel, out_shape=[S(cotangent.shape, bf16), S((rows,...  50 us
    pallas_call x1, Pallas kernels, attn_forward(): pl.pallas_call(attn_forward_kernel, out_shape=[S((rows, dim), bf16), S((r...  35.8 us

profile of v2, /device:TPU:0, one launch (start us, length us, event | category | flops | bytes accessed | tf_op | source)
XLA Modules:
  0.0 373.6 jit_solution(13614390530300072316)
XLA Ops:
  0.7 1.6 reshape.116.refs_3_
  2.3 1.7 reshape.117.refs_4_
  4.0 1.7 reshape.114.refs_1_
  15.8 0.7 pad.82
  17.3 1.4 reshape.115.refs_2_
  18.7 93.2 %gather.1 = (bf16[8,2,2,16,128]{4,3,2,1,0:T(8,128)(2,1)}, bf16[8,2,2,24,2304]{4,3,2,1,0:T(8,128)(2,1)}, bf16[8,2,2,24,768]{4,3,2,1,0:T(8,128)(2,1)}, bf16[8,2,2,...) custom-call(bf16[16,128]{1,0:T(8,128)(2,1)} %pad_bitcast_fusion.refs_0_, bf16[24,2304]{1,0:T(8,128)(2,1)} %reshape.114.refs_1_, ...), custom_call_target="tpu_custom_call" | custom-call | tf_op jit(solution)/shard_map/gather/pallas_call | solution.py:383
  111.9 0.9 bitcast_convert_fusion
  115.1 1.0 copy.44.mask
  116.1 35.8 %attn_fwd.1 = (bf16[1000,768]{1,0:T(8,128)(2,1)}, bf16[1000,2304]{1,0:T(8,128)(2,1)}, bf16[60,200,200]{2,1,0:T(8,128)(2,1)}, bf16[1000,768]{1,0:T(8,128)(2,1)}, ...) custom-call(bf16[5,197,768]{2,1,0:T(8,128)(2,1)} %patches.3, f32[5,197,1]{2,1,0:T(8,128)} %copy.44.mask, f32[16,768]{1,0:T(8,128)} %pad.84.vecs, ...), custom_call_target="tpu_custom_call" | custom-call | tf_op jit(solution)/shard_map/attn_fwd/pallas_call | solution.py:590
  151.9 0.7 reshape_squeeze.3.up_b
  152.5 50.0 %mlp.1 = (bf16[5,197,768]{2,1,0:T(8,128)(2,1)}, f32[1000,768]{1,0:T(8,128)}, bf16[768,3072]{1,0:T(8,128)(2,1)}, bf16[3072,768]{1,0:T(8,128)(2,1)}, f32[16,768]{1,0:T(8,128)}, /*index=5*/f32[1,3072]{1,0:T(1,128)}) custom-call(f32[1000,768]{1,0:T(8,128)} %get-tuple-element.49.middle, bf16[5,197,768]{2,1,0:T(8,128)(2,1)} %cotangent.1, f32[5,197,1]{2,1,0:T(8,128)} %copy.44.mask, ...), custom_call_target="tpu_custom_call" | custom-call | tf_op jit(solution)/shard_map/mlp/pallas_call | solution.py:684
  202.5 50.9 %attn_bwd.1 = (bf16[5,197,768]{2,1,0:T(8,128)(2,1)}, bf16[768,2304]{1,0:T(8,128)(2,1)}, bf16[768,768]{1,0:T(8,128)(2,1)}, f32[16,768]{1,0:T(8,128)}, f32[16,768]{1,0:T(8,128)}) custom-call(f32[1000,768]{1,0:T(8,128)} %get-tuple-element.53.grad_middle, f32[1000,768]{1,0:T(8,128)} %get-tuple-element.54.branch, bf16[1000,768]{1,0:T(8,128)(2,1)} %get-tuple-element.55.att, ...), custom_call_target="tpu_custom_call" | custom-call | tf_op jit(solution)/shard_map/attn_bwd/pallas_call | solution.py:844
  253.4 0.7 slice.71
  254.1 0.8 slice.72
  255.2 0.8 slice_bitcast_fusion
  258.0 0.8 pad_maximum_fusion.refs_4_
  258.7 104.3 %reduce.5 = (f32[24,2304]{1,0:T(8,128)}, f32[24,768]{1,0:T(8,128)}, f32[24,3072]{1,0:T(8,128)}, f32[96,768]{1,0:T(8,128)}, f32[16,128]{1,0:T(8,128)}) custom-call(bf16[8,2,2,24,2304]{4,3,2,1,0:T(8,128)(2,1)} %bitcast.70, bf16[8,2,2,24,768]{4,3,2,1,0:T(8,128)(2,1)} %bitcast.72, bf16[8,2,2,24,3072]{4,3,2,1,0:T(8,128)(2,1)} %bitcast.64, ...), custom_call_target="tpu_custom_call" | custom-call | tf_op jit(solution)/shard_map/reduce/pallas_call | solution.py:418
  363.1 1.7 copy.54
  364.8 1.7 reshape.134
  366.5 1.6 reshape.130
  368.1 1.5 reshape.132
  369.7 1.5 slice_bitcast_fusion.2
  371.2 1.3 slice_bitcast_fusion.1
  372.4 1.2 slice_bitcast_fusion.4
  (57 shorter events, 15.2 us)
Async XLA Ops:
  0.7 114.4 %copy-start.1 = (s32[5,197]{1,0:T(8,128)S(1)}, s32[5,197]{1,0:T(8,128)}, u32[]{:S(2)}) copy-start(s32[5,197]{1,0:T(8,128)} %param.21) | copy-start | bytes 11824
  202.5 54.7 %copy-start = (f32[1,3072]{1,0:T(1,128)S(1)}, f32[1,3072]{1,0:T(1,128)}, u32[]{:S(2)}) copy-start(f32[1,3072]{1,0:T(1,128)} %get-tuple-element.66) | copy-start | bytes 36868
